TPU v7x, 32 devices: a whole 2x2x4 slice. The times are simulated.
32 devices in a mesh: dp: 8 (over y, x, core), seq: 4 (over z).
Axes of the slice: x: 2, y: 2, z: 4, core: 2. Of those that a mesh axis runs over, the one named last changes fastest.
Arguments:
- tokens: bfloat16 [2, 8, 2048, 768], P(None, 'dp', 'seq'), may hold values from -6 to 6
- seq_lengths: int32 [2, 8], P(None, 'dp'), may hold values from 512 to 2048, as said below
- query_weight: bfloat16 [768, 768], P(('dp', 'seq')), may hold values from -0.21875 to 0.21875
- query_bias: bfloat16 [768], P(('dp', 'seq')), may hold values from -3 to 3
- key_weight: bfloat16 [768, 768], P(('dp', 'seq')), may hold values from -0.21875 to 0.21875
- key_bias: bfloat16 [768], P(('dp', 'seq')), may hold values from -3 to 3
- value_weight: bfloat16 [768, 768], P(('dp', 'seq')), may hold values from -0.21875 to 0.21875
- value_bias: bfloat16 [768], P(('dp', 'seq')), may hold values from -3 to 3
- output_weight: bfloat16 [768, 768], P(('dp', 'seq')), may hold values from -1.25 to 1.25
- output_bias: bfloat16 [768], P(('dp', 'seq')), may hold values from -3 to 3
- gain_first: bfloat16 [768], P(('dp', 'seq')), may hold values from 0.5 to 1.5
- shift_first: bfloat16 [768], P(('dp', 'seq')), may hold values from -3 to 3
- inner_weight: bfloat16 [768, 3072], P(('dp', 'seq')), may hold values from -0.21875 to 0.21875
- inner_bias: bfloat16 [3072], P(('dp', 'seq')), may hold values from -3 to 3
- outer_weight: bfloat16 [3072, 768], P(('dp', 'seq')), may hold values from -0.109375 to 0.109375
- outer_bias: bfloat16 [768], P(('dp', 'seq')), may hold values from -3 to 3
- gain_second: bfloat16 [768], P(('dp', 'seq')), may hold values from 0.5 to 1.5
- shift_second: bfloat16 [768], P(('dp', 'seq')), may hold values from -3 to 3
- cotangent: bfloat16 [2, 8, 2048, 768], P(None, 'dp', 'seq'), may hold values from -6 to 6
Outputs:
- layer_out: bfloat16 [2, 8, 2048, 768], P(None, 'dp', 'seq')
- grad_tokens: float32 [2, 8, 2048, 768], P(None, 'dp', 'seq')
- grad_query_weight: float32 [768, 768], P(('dp', 'seq'))
- grad_query_bias: float32 [768], P(('dp', 'seq'))
- grad_key_weight: float32 [768, 768], P(('dp', 'seq'))
- grad_key_bias: float32 [768], P(('dp', 'seq'))
- grad_value_weight: float32 [768, 768], P(('dp', 'seq'))
- grad_value_bias: float32 [768], P(('dp', 'seq'))
- grad_output_weight: float32 [768, 768], P(('dp', 'seq'))
- grad_output_bias: float32 [768], P(('dp', 'seq'))
- grad_gain_first: float32 [768], P(('dp', 'seq'))
- grad_shift_first: float32 [768], P(('dp', 'seq'))
- grad_inner_weight: float32 [768, 3072], P(('dp', 'seq'))
- grad_inner_bias: float32 [3072], P(('dp', 'seq'))
- grad_outer_weight: float32 [3072, 768], P(('dp', 'seq'))
- grad_outer_bias: float32 [768], P(('dp', 'seq'))
- grad_gain_second: float32 [768], P(('dp', 'seq'))
- grad_shift_second: float32 [768], P(('dp', 'seq'))
Inputs may be any that keep to these rules, and one draw needn't show every extreme that they name: `seq_lengths`: in every micro-batch some sequence has exactly 2048 valid positions; positions at or past a sequence's length are padding.
All inputs are finite; a program needn't handle non-finite values.
Results may differ from a plain program's by a relative error of at most 0.014.
Values may be sent and summed in bfloat16 or wider, within the bound.
No kernel may reach another device: no remote copies, remote signals or barrier semaphores. Data moves between devices by JAX's collectives and lax.ppermute only.
A program may use at most 192 MiB of HBM per device.

v0:
```python
import math

import jax
import jax.numpy as jnp
from jax import lax
from jax.sharding import PartitionSpec as P

H = 12
HD = 64
BLOCK = 512


NORM_EPS = 1e-05
HALF_TURN = math.pi / 2


def layer_norm(values, norm_gain, norm_shift):
    center = values - jnp.mean(values, axis=-1, keepdims=True)
    spread = jnp.mean(center * center, axis=-1, keepdims=True)
    return center * lax.rsqrt(spread + NORM_EPS) * norm_gain + norm_shift


def reweight(places, limit):
    angle = HALF_TURN * places[:, None] / limit[None, :]
    live = (places[:, None] < limit[None, :]).astype(jnp.float32)
    return (jnp.cos(angle) * live, jnp.sin(angle) * live)


def attention(queries, key_rows, values, lengths, offset, initial):
    total_rows, head_count, head_size = queries.shape
    block_rows = min(BLOCK, total_rows)
    block_count = total_rows // block_rows
    limit = lengths.astype(jnp.float32)
    causal = jnp.tril(jnp.ones((block_rows, block_rows), jnp.float32))
    highest = lax.Precision.HIGHEST

    def attend(state_now, inputs):
        sum_cos, sum_sin, norm_cos, norm_sin = state_now
        query_blk, key_blk, value_blk, block_index = inputs
        places = (offset + block_index * block_rows + jnp.arange(block_rows)).astype(jnp.float32)
        weight_cos, weight_sin = reweight(places, limit)
        query_relu = jax.nn.relu(query_blk)
        key_relu = jax.nn.relu(key_blk)
        query_cos = query_relu * weight_cos[:, :, None]
        query_sin = query_relu * weight_sin[:, :, None]
        key_cos = key_relu * weight_cos[:, :, None]
        key_sin = key_relu * weight_sin[:, :, None]
        scores = jnp.einsum("igd,jgd->gij", query_cos, key_cos, precision=highest)
        scores = scores + jnp.einsum("igd,jgd->gij", query_sin, key_sin, precision=highest)
        scores = scores * causal[None, :, :]
        numer = jnp.einsum("gij,jge->ige", scores, value_blk, precision=highest)
        numer = numer + jnp.einsum("igd,gde->ige", query_cos, sum_cos, precision=highest)
        numer = numer + jnp.einsum("igd,gde->ige", query_sin, sum_sin, precision=highest)
        denom = jnp.sum(scores, axis=2).T
        denom = denom + jnp.einsum("igd,gd->ig", query_cos, norm_cos, precision=highest)
        denom = denom + jnp.einsum("igd,gd->ig", query_sin, norm_sin, precision=highest)
        output = numer / jnp.maximum(denom, 1.0)[:, :, None]
        sum_cos = sum_cos + jnp.einsum("jgd,jge->gde", key_cos, value_blk, precision=highest)
        sum_sin = sum_sin + jnp.einsum("jgd,jge->gde", key_sin, value_blk, precision=highest)
        norm_cos = norm_cos + jnp.sum(key_cos, axis=0)
        norm_sin = norm_sin + jnp.sum(key_sin, axis=0)
        return ((sum_cos, sum_sin, norm_cos, norm_sin), output)

    stacked = (
        queries.reshape(block_count, block_rows, head_count, head_size),
        key_rows.reshape(block_count, block_rows, head_count, head_size),
        values.reshape(block_count, block_rows, head_count, head_size),
        jnp.arange(block_count),
    )
    final_state, outputs = lax.scan(jax.checkpoint(attend), initial, stacked)
    return outputs.reshape(total_rows, head_count, head_size)


def make_state(head_count):
    return (
        jnp.zeros((head_count, HD, HD), jnp.float32),
        jnp.zeros((head_count, HD, HD), jnp.float32),
        jnp.zeros((head_count, HD), jnp.float32),
        jnp.zeros((head_count, HD), jnp.float32),
    )


def head_view(packed):
    return packed.astype(jnp.float32)


def per_device(
    tokens,
    seq_lengths,
    query_weight,
    query_bias,
    key_weight,
    key_bias,
    value_weight,
    value_bias,
    output_weight,
    output_bias,
    gain_first,
    shift_first,
    inner_weight,
    inner_bias,
    outer_weight,
    outer_bias,
    gain_second,
    shift_second,
    cotangent,
):
    seq_count = lax.axis_size("seq")
    micro_count, seqs_here, shard_rows, width = tokens.shape
    item_count = seqs_here * H
    item_share = item_count // seq_count
    seq_place = lax.axis_index("seq")
    token_count = seqs_here * shard_rows
    item_index = seq_place * item_share + jnp.arange(item_share)
    head_owner = item_index // H
    owner_match = head_owner[:, None] == jnp.arange(seqs_here)[None, :]
    totals = None
    layer_rows = []
    input_grads = []
    for batch_index in range(micro_count):
        weights_now = (
            lax.all_gather(query_weight, ("dp", "seq"), axis=0, tiled=True),
            lax.all_gather(query_bias, ("dp", "seq"), axis=0, tiled=True),
            lax.all_gather(key_weight, ("dp", "seq"), axis=0, tiled=True),
            lax.all_gather(key_bias, ("dp", "seq"), axis=0, tiled=True),
            lax.all_gather(value_weight, ("dp", "seq"), axis=0, tiled=True),
            lax.all_gather(value_bias, ("dp", "seq"), axis=0, tiled=True),
            lax.all_gather(output_weight, ("dp", "seq"), axis=0, tiled=True),
            lax.all_gather(output_bias, ("dp", "seq"), axis=0, tiled=True),
            lax.all_gather(gain_first, ("dp", "seq"), axis=0, tiled=True),
            lax.all_gather(shift_first, ("dp", "seq"), axis=0, tiled=True),
            lax.all_gather(inner_weight, ("dp", "seq"), axis=0, tiled=True),
            lax.all_gather(inner_bias, ("dp", "seq"), axis=0, tiled=True),
            lax.all_gather(outer_weight, ("dp", "seq"), axis=0, tiled=True),
            lax.all_gather(outer_bias, ("dp", "seq"), axis=0, tiled=True),
            lax.all_gather(gain_second, ("dp", "seq"), axis=0, tiled=True),
            lax.all_gather(shift_second, ("dp", "seq"), axis=0, tiled=True),
        )
        (
            w_query,
            b_query,
            w_key,
            b_key,
            w_value,
            b_value,
            w_output,
            b_output,
            gain_one,
            shift_one,
            w_inner,
            b_inner,
            w_outer,
            b_outer,
            gain_two,
            shift_two,
        ) = weights_now
        lengths_now = seq_lengths[batch_index]
        head_lengths = jnp.sum(jnp.where(owner_match, lengths_now[None, :], 0), axis=1)
        token_now = tokens[batch_index]

        def project(weight_full, bias_full):
            product = jnp.einsum(
                "srd,de->rse", token_now, weight_full, preferred_element_type=jnp.float32
            )
            return (product + bias_full.astype(jnp.float32)).astype(jnp.bfloat16)

        query_low = project(w_query, b_query)
        key_low = project(w_key, b_key)
        value_low = project(w_value, b_value)
        moved = (
            lax.all_to_all(
                query_low.reshape(shard_rows, item_count, HD),
                "seq",
                split_axis=1,
                concat_axis=0,
                tiled=True,
            ),
            lax.all_to_all(
                key_low.reshape(shard_rows, item_count, HD),
                "seq",
                split_axis=1,
                concat_axis=0,
                tiled=True,
            ),
            lax.all_to_all(
                value_low.reshape(shard_rows, item_count, HD),
                "seq",
                split_axis=1,
                concat_axis=0,
                tiled=True,
            ),
        )
        zero_state = make_state(item_share)

        def core_heads(query_in, key_in, value_in):
            return attention(query_in, key_in, value_in, head_lengths, 0, zero_state)

        mixed_heads, attention_pull = jax.vjp(
            core_heads, head_view(moved[0]), head_view(moved[1]), head_view(moved[2])
        )
        mixed_send = mixed_heads.astype(jnp.bfloat16)
        mixed_low = lax.all_to_all(
            mixed_send, "seq", split_axis=0, concat_axis=1, tiled=True
        ).reshape(shard_rows, seqs_here, width)
        attended = jnp.einsum(
            "rse,ef->srf", mixed_low, w_output, preferred_element_type=jnp.float32
        )
        attended = attended + b_output.astype(jnp.float32)
        resid_one = token_now.astype(jnp.float32) + attended
        first, norm_one_pull = jax.vjp(
            layer_norm, resid_one, gain_one.astype(jnp.float32), shift_one.astype(jnp.float32)
        )
        first_flat = first.reshape(token_count, width)
        first_low = first_flat.astype(jnp.bfloat16)
        inner = jnp.dot(first_low, w_inner, preferred_element_type=jnp.float32) + b_inner.astype(
            jnp.float32
        )
        hidden_full, gelu_pull = jax.vjp(jax.nn.gelu, inner)
        hidden = hidden_full.astype(jnp.bfloat16)
        outer = jnp.dot(hidden, w_outer, preferred_element_type=jnp.float32) + b_outer.astype(
            jnp.float32
        )
        final, norm_two_pull = jax.vjp(
            layer_norm,
            first_flat + outer,
            gain_two.astype(jnp.float32),
            shift_two.astype(jnp.float32),
        )
        layer_rows.append(final.astype(jnp.bfloat16).reshape(seqs_here, shard_rows, width))
        grad_final = cotangent[batch_index].astype(jnp.float32).reshape(token_count, width)
        d_second, grad_gain_two, grad_shift_two = norm_two_pull(grad_final)
        d_outer = d_second.astype(jnp.bfloat16)
        grad_w_outer = jnp.einsum("nf,nd->fd", hidden, d_outer, preferred_element_type=jnp.float32)
        grad_b_outer = jnp.sum(d_outer, axis=0, dtype=jnp.float32)
        d_hidden = jnp.einsum("nd,fd->nf", d_outer, w_outer, preferred_element_type=jnp.float32)
        (d_inner_full,) = gelu_pull(d_hidden)
        d_inner = d_inner_full.astype(jnp.bfloat16)
        grad_w_inner = jnp.einsum(
            "nd,nf->df", first_low, d_inner, preferred_element_type=jnp.float32
        )
        grad_b_inner = jnp.sum(d_inner, axis=0, dtype=jnp.float32)
        d_first = d_second + jnp.einsum(
            "nf,df->nd", d_inner, w_inner, preferred_element_type=jnp.float32
        )
        d_resid, grad_gain_one, grad_shift_one = norm_one_pull(
            d_first.reshape(seqs_here, shard_rows, width)
        )
        d_attended = d_resid.astype(jnp.bfloat16)
        grad_w_output = jnp.einsum(
            "rse,srf->ef", mixed_low, d_attended, preferred_element_type=jnp.float32
        )
        grad_b_output = jnp.sum(d_attended, axis=(0, 1), dtype=jnp.float32)
        d_mixed = jnp.einsum(
            "srf,ef->rse", d_attended, w_output, preferred_element_type=jnp.float32
        ).astype(jnp.bfloat16)
        d_heads = lax.all_to_all(
            d_mixed.reshape(shard_rows, item_count, HD),
            "seq",
            split_axis=1,
            concat_axis=0,
            tiled=True,
        )
        d_query_heads, d_key_heads, d_value_heads = attention_pull(head_view(d_heads))
        returned = (
            lax.all_to_all(
                d_query_heads.astype(jnp.bfloat16), "seq", split_axis=0, concat_axis=1, tiled=True
            ),
            lax.all_to_all(
                d_key_heads.astype(jnp.bfloat16), "seq", split_axis=0, concat_axis=1, tiled=True
            ),
            lax.all_to_all(
                d_value_heads.astype(jnp.bfloat16), "seq", split_axis=0, concat_axis=1, tiled=True
            ),
        )
        d_query = returned[0].reshape(shard_rows, seqs_here, width)
        d_key = returned[1].reshape(shard_rows, seqs_here, width)
        d_value = returned[2].reshape(shard_rows, seqs_here, width)
        grad_w_query = jnp.einsum(
            "srd,rse->de", token_now, d_query, preferred_element_type=jnp.float32
        )
        grad_w_key = jnp.einsum("srd,rse->de", token_now, d_key, preferred_element_type=jnp.float32)
        grad_w_value = jnp.einsum(
            "srd,rse->de", token_now, d_value, preferred_element_type=jnp.float32
        )
        grad_b_query = jnp.sum(d_query, axis=(0, 1), dtype=jnp.float32)
        grad_b_key = jnp.sum(d_key, axis=(0, 1), dtype=jnp.float32)
        grad_b_value = jnp.sum(d_value, axis=(0, 1), dtype=jnp.float32)
        d_tokens = d_resid + jnp.einsum(
            "rse,de->srd", d_query, w_query, preferred_element_type=jnp.float32
        )
        d_tokens = d_tokens + jnp.einsum(
            "rse,de->srd", d_key, w_key, preferred_element_type=jnp.float32
        )
        d_tokens = d_tokens + jnp.einsum(
            "rse,de->srd", d_value, w_value, preferred_element_type=jnp.float32
        )
        input_grads.append(d_tokens)
        batch_grads = (
            grad_w_query,
            grad_b_query,
            grad_w_key,
            grad_b_key,
            grad_w_value,
            grad_b_value,
            grad_w_output,
            grad_b_output,
            grad_gain_one,
            grad_shift_one,
            grad_w_inner,
            grad_b_inner,
            grad_w_outer,
            grad_b_outer,
            grad_gain_two,
            grad_shift_two,
        )
        if totals is None:
            totals = batch_grads
        else:
            totals = jax.tree.map(jnp.add, totals, batch_grads)
    shards = (
        lax.psum_scatter(totals[0], ("dp", "seq"), scatter_dimension=0, tiled=True),
        lax.psum_scatter(totals[1], ("dp", "seq"), scatter_dimension=0, tiled=True),
        lax.psum_scatter(totals[2], ("dp", "seq"), scatter_dimension=0, tiled=True),
        lax.psum_scatter(totals[3], ("dp", "seq"), scatter_dimension=0, tiled=True),
        lax.psum_scatter(totals[4], ("dp", "seq"), scatter_dimension=0, tiled=True),
        lax.psum_scatter(totals[5], ("dp", "seq"), scatter_dimension=0, tiled=True),
        lax.psum_scatter(totals[6], ("dp", "seq"), scatter_dimension=0, tiled=True),
        lax.psum_scatter(totals[7], ("dp", "seq"), scatter_dimension=0, tiled=True),
        lax.psum_scatter(totals[8], ("dp", "seq"), scatter_dimension=0, tiled=True),
        lax.psum_scatter(totals[9], ("dp", "seq"), scatter_dimension=0, tiled=True),
        lax.psum_scatter(totals[10], ("dp", "seq"), scatter_dimension=0, tiled=True),
        lax.psum_scatter(totals[11], ("dp", "seq"), scatter_dimension=0, tiled=True),
        lax.psum_scatter(totals[12], ("dp", "seq"), scatter_dimension=0, tiled=True),
        lax.psum_scatter(totals[13], ("dp", "seq"), scatter_dimension=0, tiled=True),
        lax.psum_scatter(totals[14], ("dp", "seq"), scatter_dimension=0, tiled=True),
        lax.psum_scatter(totals[15], ("dp", "seq"), scatter_dimension=0, tiled=True),
    )
    return (jnp.stack(layer_rows), jnp.stack(input_grads)) + tuple(shards)


def solution(mesh):
    in_specs = (
        P(None, "dp", "seq", None),
        P(None, "dp"),
        P(("dp", "seq"), None),
        P(("dp", "seq")),
        P(("dp", "seq"), None),
        P(("dp", "seq")),
        P(("dp", "seq"), None),
        P(("dp", "seq")),
        P(("dp", "seq"), None),
        P(("dp", "seq")),
        P(("dp", "seq")),
        P(("dp", "seq")),
        P(("dp", "seq"), None),
        P(("dp", "seq")),
        P(("dp", "seq"), None),
        P(("dp", "seq")),
        P(("dp", "seq")),
        P(("dp", "seq")),
        P(None, "dp", "seq", None),
    )
    out_specs = (
        P(None, "dp", "seq", None),
        P(None, "dp", "seq", None),
        P(("dp", "seq"), None),
        P(("dp", "seq")),
        P(("dp", "seq"), None),
        P(("dp", "seq")),
        P(("dp", "seq"), None),
        P(("dp", "seq")),
        P(("dp", "seq"), None),
        P(("dp", "seq")),
        P(("dp", "seq")),
        P(("dp", "seq")),
        P(("dp", "seq"), None),
        P(("dp", "seq")),
        P(("dp", "seq"), None),
        P(("dp", "seq")),
        P(("dp", "seq")),
        P(("dp", "seq")),
    )
    return jax.shard_map(
        per_device, mesh=mesh, in_specs=in_specs, out_specs=out_specs, check_vma=False
    )
```

profile of v0, /device:TPU:0, one launch (start us, length us, event | category | flops | bytes accessed | tf_op | source)
XLA Modules:
  0.0 1656.1 jit_solution(1364522023092862360)
XLA Ops:
  19.0 42.7 %all-reduce.21 = (bf16[768]{0:T(1024)(128)(2,1)S(1)}, bf16[768]{0:T(1024)(128)(2,1)S(1)}, bf16[768]{0:T(1024)(128)(2,1)S(1)}, bf16[768]{0:T(1024)(128)(2,1)}, bf...) all-reduce(bf16[768]{0:T(1024)(128)(2,1)S(1)} %dynamic-update-slice, ...), channel_id=1, replica_groups=mesh['dp'=8,'seq'=4] {'dp','seq'}, use_global_device_ids=true, to_apply=%add | all-reduce | flops 9984 | bytes 39936
  61.6 6.1 all-gather.9.cloned.1.call-done
  74.6 53.0 %all-gather.7.cloned.1.call-done = bf16[768,768]{1,0:T(8,128)(2,1)} async-done(((bf16[24,768]{1,0:T(8,128)(2,1)}), bf16[768,768]{1,0:T(8,128)(2,1)}) %all-gather.7.cloned.1.call-update) | async-done | bytes 1179664 | tf_op jit(solution)/shard_map/all_gather | solution.py:124
  130.6 4.2 all-to-all-start.4
  134.8 52.8 %all-gather.11.cloned.1.call-done = bf16[768,768]{1,0:T(8,128)(2,1)} async-done(((bf16[24,768]{1,0:T(8,128)(2,1)}), bf16[768,768]{1,0:T(8,128)(2,1)}) %all-gather.11.cloned.1.call-update) | async-done | bytes 1179664 | tf_op jit(solution)/shard_map/all_gather | solution.py:122
  190.6 4.3 all-to-all-start.6
  196.6 19.9 %all-to-all-done.6 = bf16[512,12,64]{0,2,1:T(8,128)(2,1)} async-done(((bf16[512,12,64]{0,2,1:T(8,128)(2,1)}), bf16[512,12,64]{0,2,1:T(8,128)(2,1)}, u32[]{:S(2)}, u32[]{:S(2)}) %all-to-all-start.6) | async-done | bytes 786464 | tf_op jit(solution)/shard_map/all_to_all | solution.py:171
  223.6 17.4 %all-to-all-done.1 = bf16[512,12,64]{0,2,1:T(8,128)(2,1)S(1)} async-done(((bf16[512,12,64]{0,2,1:T(8,128)(2,1)}), bf16[512,12,64]{0,2,1:T(8,128)(2,1)S(1)}, u32[]{:S(2)}, u32[]{:S(2)}) %all-to-all-start.1) | async-done | bytes 786464 | tf_op jit(solution)/shard_map/all_to_all | solution.py:185
  254.7 11.4 all-to-all-done
  266.1 4.4 all-to-all-start.2
  274.3 109.1 %while.111 = (s32[]{:T(128)}, f32[3,64,64]{2,1,0:T(8,128)S(1)}, f32[3,64,64]{2,1,0:T(8,128)S(1)}, f32[3,64]{1,0:T(4,128)}, f32[3,64]{1,0:T(4,128)}, /*index=5*/b...) while((s32[]{:T(128)}, f32[3,64,64]{2,1,0:T(8,128)S(1)}, ...), condition=%wide.region_13.14_spmd.clone, body=%wide.region_9.13_spmd.clone.sunk | while | flops 2122035456 | bytes 35606024 | solution.py:70
  280.3 4.7 fusion.642
  307.0 4.7 fusion.642
  334.5 4.7 fusion.642
  362.0 4.8 fusion.642
  391.5 5.6 all-to-all-start.7
  402.3 92.9 %while.110 = (s32[]{:T(128)}, f32[3,64,64]{2,1,0:T(8,128)S(1)}, f32[3,64,64]{2,1,0:T(8,128)S(1)}, f32[3,64]{1,0:T(4,128)S(1)}, f32[3,64]{1,0:T(4,128)S(1)}, /*in...) while((s32[]{:T(128)}, f32[3,64,64]{2,1,0:T(8,128)S(1)}, ...), condition=%wide.region_4.5_spmd.clone, body=%wide.region_0.0_spmd.clone.sunk | while | flops 2122035456 | bytes 35605332 | solution.py:70
  500.6 5.3 all-to-all-start.3
  511.2 13.5 all-to-all-done.3
  537.9 7.0 fusion.388
  544.9 7.9 fusion.404
  557.1 4.2 fusion.402
  568.8 4.5 fusion.410
  573.3 18.0 %convert_reduce_fusion.1 = (f32[3072]{0:T(1024)}, bf16[512,3072]{1,0:T(8,128)(2,1)}, f32[3072]{0:T(1024)}, bf16[512,3072]{1,0:T(8,128)(2,1)S(1)}) fusion(f32[512,3072]{1,0:T(8,128)} %copy-done.110, f32[3072]{0:T(1024)S(1)} %convert_element_type.481, f32[512,3072]{1,0:T(8,128)} %fusion.410, f32[512,3072]{1,0:T(8,128)} %fusion.388, ...), kind=kOutput, calls=%fused_computation.463 | convolution fusion | flops 2488264704 | bytes 30707712 | tf_op jit(solution)/shard_map/nd,fd->nf/dot_general | solution.py:235
  616.4 11.5 all-to-all-done.8
  627.9 4.2 all-to-all-start.12
  636.5 173.0 %while.112 = (s32[]{:T(128)}, f32[3,64,64]{2,1,0:T(8,128)S(1)}, f32[3,64,64]{2,1,0:T(8,128)S(1)}, f32[3,64]{1,0:T(4,128)S(1)}, f32[3,64]{1,0:T(4,128)S(1)}, /*in...) while((s32[]{:T(128)}, f32[3,64,64]{2,1,0:T(8,128)S(1)}, ...), condition=%wide.region_25.26_spmd.clone, body=%wide.region_22.25_spmd.clone.sunk | while | flops 6211543040 | bytes 82320360 | solution.py:70
  814.9 5.0 all-to-all-start.11
  825.4 183.5 %while.113 = (s32[]{:T(128)}, f32[3,64,64]{2,1,0:T(8,128)S(1)}, f32[3,64,64]{2,1,0:T(8,128)S(1)}, f32[3,64]{1,0:T(4,128)S(1)}, f32[3,64]{1,0:T(4,128)S(1)}, /*in...) while((s32[]{:T(128)}, f32[3,64,64]{2,1,0:T(8,128)S(1)}, ...), condition=%wide.region_33.34_spmd.clone, body=%wide.region_30.33_spmd.clone.sunk | while | flops 6211543040 | bytes 82320360 | solution.py:70
  1014.3 5.1 all-to-all-start.15
  1024.5 13.5 all-to-all-done.15
  1055.0 4.2 reshape.1171
  1067.4 4.2 reshape.1165
  1071.6 11.5 all-to-all-done.10
  1083.1 4.2 all-to-all-start.14
  1095.4 17.3 %all-to-all-done.14 = bf16[4,2,49152]{2,1,0:T(2,128)(2,1)} async-done(((bf16[4,2,49152]{2,1,0:T(2,128)(2,1)}), bf16[4,2,49152]{2,1,0:T(2,128)(2,1)}, u32[]{:S(2)}, u32[]{:S(2)}) %all-to-all-start.14) | async-done | bytes 786464 | tf_op jit(solution)/shard_map/all_to_all | solution.py:268
  1145.0 4.2 reshape.1167
  1149.2 11.8 all-to-all-done.9
  1161.0 4.2 all-to-all-start.13
  1173.3 11.6 all-to-all-done.13
  1201.4 6.3 fusion.389
  1207.8 10.5 convolution_add_fusion.24
  1219.0 5.5 fusion.386
  1224.5 6.0 convolution_add_fusion.25
  1262.7 38.7 %all-reduce.20 = (f32[768]{0:T(1024)S(1)}, f32[768]{0:T(1024)S(1)}, f32[768]{0:T(1024)S(1)}, f32[768]{0:T(1024)S(1)}, f32[768]{0:T(1024)S(1)}, /*index=5*/f32[76...) all-reduce(f32[768]{0:T(1024)S(1)} %add.724, ...), channel_id=3, replica_groups=mesh['dp'=8,'seq'=4] {'dp','seq'}, use_global_device_ids=true, to_apply=%region_37.38.clone | all-reduce | flops 9984 | bytes 79872
  1319.1 46.5 %reduce-scatter.19.cloned.1.call-done = f32[24,768]{1,0:T(8,128)} async-done(((f32[768,768]{1,0:T(8,128)}), f32[24,768]{1,0:T(8,128)}) %reduce-scatter.19.cloned.1.call-update) | async-done | bytes 73744
  1365.5 141.8 %reduce-scatter.17.cloned.1.call-done = f32[96,768]{1,0:T(8,128)} async-done(((f32[3072,768]{1,0:T(8,128)}), f32[96,768]{1,0:T(8,128)}) %reduce-scatter.17.cloned.1.call-update) | async-done | bytes 294928 | tf_op jit(solution)/shard_map/reduce_scatter | solution.py:333
  1507.3 141.4 %reduce-scatter.15.cloned.1.call-done = f32[24,3072]{1,0:T(8,128)} async-done(((f32[768,3072]{1,0:T(8,128)}), f32[24,3072]{1,0:T(8,128)}) %reduce-scatter.15.cloned.1.call-update) | async-done | bytes 294928 | tf_op jit(solution)/shard_map/reduce_scatter | solution.py:331
  (1063 shorter events, 769.1 us)
Async XLA Ops:
  7.2 60.5 %all-gather.9.cloned.1.call-start = ((), (), s32[]{:S(2)}) async-start(), calls=%async_computation.23 | async-start | bytes 1216512 | tf_op jit(solution)/shard_map/all_gather | solution.py:126
  7.9 119.6 %all-gather.7.cloned.1.call-start = ((), (), s32[]{:S(2)}) async-start(), calls=%async_computation.22 | async-start | bytes 1216512 | tf_op jit(solution)/shard_map/all_gather | solution.py:124
  8.7 178.9 %all-gather.11.cloned.1.call-start = ((), (), s32[]{:S(2)}) async-start(), calls=%async_computation.24 | async-start | bytes 1216512 | tf_op jit(solution)/shard_map/all_gather | solution.py:122
  9.4 521.8 %all-gather.13.cloned.1.call-start = ((), (), s32[]{:S(2)}) async-start(), calls=%async_computation.25 | async-start | bytes 1216512 | tf_op jit(solution)/shard_map/all_gather | solution.py:128
  10.0 528.0 %all-gather.15.cloned.1.call-start = ((), (), s32[]{:S(2)}) async-start(), calls=%async_computation.26 | async-start | bytes 4866048 | tf_op jit(solution)/shard_map/all_gather | solution.py:132
  70.9 56.7 %copy-start.6 = (bf16[2,1,512,768]{3,2,1,0:T(8,128)(2,1)S(1)}, bf16[2,1,512,768]{3,2,1,0:T(8,128)(2,1)}, u32[]{:S(2)}) copy-start(bf16[2,1,512,768]{3,2,1,0:T(8,128)(2,1)} %param.27) | copy-start | bytes 4718596
  70.9 59.6 %all-to-all-start.5 = ((bf16[512,12,64]{0,2,1:T(8,128)(2,1)}), bf16[512,12,64]{0,2,1:T(8,128)(2,1)S(1)}, u32[]{:S(2)}, u32[]{:S(2)}) async-start(bf16[512,12,64]{0,2,1:T(8,128)(2,1)} %bitcast.37), calls=%async_computation.5 | async-start | bytes 1572864 | tf_op jit(solution)/shard_map/all_to_all | solution.py:185
  130.6 57.0 %copy-start.33 = (bf16[512,12,64]{0,2,1:T(8,128)(2,1)}, bf16[512,12,64]{0,2,1:T(8,128)(2,1)S(1)}, u32[]{:S(2)}) copy-start(bf16[512,12,64]{0,2,1:T(8,128)(2,1)S(1)} %all-to-all-done.5) | copy-start | bytes 2359300
  130.6 60.0 %all-to-all-start.4 = ((bf16[512,12,64]{0,2,1:T(8,128)(2,1)}), bf16[512,12,64]{0,2,1:T(8,128)(2,1)}, u32[]{:S(2)}, u32[]{:S(2)}) async-start(bf16[512,12,64]{0,2,1:T(8,128)(2,1)} %bitcast.32), calls=%async_computation.4 | async-start | bytes 1572864 | tf_op jit(solution)/shard_map/all_to_all | solution.py:178
  190.6 26.0 %all-to-all-start.6 = ((bf16[512,12,64]{0,2,1:T(8,128)(2,1)}), bf16[512,12,64]{0,2,1:T(8,128)(2,1)}, u32[]{:S(2)}, u32[]{:S(2)}) async-start(bf16[512,12,64]{0,2,1:T(8,128)(2,1)} %bitcast.1129), calls=%async_computation.6 | async-start | bytes 1572864 | tf_op jit(solution)/shard_map/all_to_all | solution.py:171
  216.5 24.5 %all-to-all-start.1 = ((bf16[512,12,64]{0,2,1:T(8,128)(2,1)}), bf16[512,12,64]{0,2,1:T(8,128)(2,1)S(1)}, u32[]{:S(2)}, u32[]{:S(2)}) async-start(bf16[512,12,64]{0,2,1:T(8,128)(2,1)} %bitcast.1128), calls=%async_computation.1 | async-start | bytes 1572864 | tf_op jit(solution)/shard_map/all_to_all | solution.py:185
  220.0 324.9 %all-gather.17.cloned.1.call-start = ((), (), s32[]{:S(2)}) async-start(), calls=%async_computation.27 | async-start | bytes 4866048 | tf_op jit(solution)/shard_map/all_gather | solution.py:134
  223.6 20.9 %copy-start.102 = (s32[2,1]{0,1:T(1,128)S(1)}, s32[2,1]{0,1:T(1,128)}, u32[]{:S(2)}) copy-start(s32[2,1]{0,1:T(1,128)} %param.28) | copy-start | bytes 28
  241.0 25.1 %all-to-all-start = ((bf16[512,12,64]{0,2,1:T(8,128)(2,1)}), bf16[512,12,64]{0,2,1:T(8,128)(2,1)S(1)}, u32[]{:S(2)}, u32[]{:S(2)}) async-start(bf16[512,12,64]{0,2,1:T(8,128)(2,1)} %bitcast.1127), calls=%async_computation | async-start | bytes 1572864 | tf_op jit(solution)/shard_map/all_to_all | solution.py:178
  266.1 125.5 %all-to-all-start.2 = ((bf16[512,12,64]{0,2,1:T(8,128)(2,1)}), bf16[512,12,64]{0,2,1:T(8,128)(2,1)}, u32[]{:S(2)}, u32[]{:S(2)}) async-start(bf16[512,12,64]{0,2,1:T(8,128)(2,1)} %bitcast.14), calls=%async_computation.2 | async-start | bytes 1572864 | tf_op jit(solution)/shard_map/all_to_all | solution.py:171
  286.7 8.4 copy-start.36
  313.5 9.1 copy-start
  313.5 9.1 copy-start.36
  340.9 9.1 copy-start
  340.9 9.1 copy-start.36
  368.4 9.1 copy-start
  368.4 9.1 copy-start.36
  391.5 109.1 %all-to-all-start.7 = ((bf16[4,2,49152]{2,1,0:T(2,128)(2,1)}), bf16[4,2,49152]{2,1,0:T(2,128)(2,1)}, u32[]{:S(2)}, u32[]{:S(2)}) async-start(bf16[4,2,49152]{2,1,0:T(2,128)(2,1)} %reshape.1161), calls=%async_computation.7 | async-start | bytes 1572864 | tf_op jit(solution)/shard_map/all_to_all | solution.py:202
  500.6 24.1 %all-to-all-start.3 = ((bf16[4,2,49152]{2,1,0:T(2,128)(2,1)}), bf16[4,2,49152]{2,1,0:T(2,128)(2,1)S(1)}, u32[]{:S(2)}, u32[]{:S(2)}) async-start(bf16[4,2,49152]{2,1,0:T(2,128)(2,1)} %reshape.1163), calls=%async_computation.3 | async-start | bytes 1572864 | tf_op jit(solution)/shard_map/all_to_all | solution.py:202
  506.0 92.5 %copy-start.64 = (f32[768]{0:T(1024)}, f32[768]{0:T(1024)S(1)}, u32[]{:S(2)}) copy-start(f32[768]{0:T(1024)S(1)} %convert_element_type.478) | copy-start | bytes 9220
  506.0 51.0 %copy-start.66 = (f32[768]{0:T(1024)}, f32[768]{0:T(1024)S(1)}, u32[]{:S(2)}) copy-start(f32[768]{0:T(1024)S(1)} %convert_element_type.479) | copy-start | bytes 9220
  506.1 67.3 %copy-start.86 = (f32[3072]{0:T(1024)}, f32[3072]{0:T(1024)S(1)}, u32[]{:S(2)}) copy-start(f32[3072]{0:T(1024)S(1)} %convert_element_type.481) | copy-start | bytes 36868
  533.8 64.8 %copy-start.4 = (f32[1,512,768]{2,1,0:T(8,128)}, f32[1,512,768]{2,1,0:T(8,128)S(1)}, u32[]{:S(2)}) copy-start(f32[1,512,768]{2,1,0:T(8,128)S(1)} %get-tuple-element.1720) | copy-start | bytes 4718596
  533.8 64.7 %copy-start.68 = (f32[512]{0:T(512)}, f32[512]{0:T(512)S(1)}, u32[]{:S(2)}) copy-start(f32[512]{0:T(512)S(1)} %broadcast_multiply_fusion.5) | copy-start | bytes 6148
  536.4 62.1 %copy-start.74 = (f32[512]{0:T(512)}, f32[512]{0:T(512)S(1)}, u32[]{:S(2)}) copy-start(f32[512]{0:T(512)S(1)} %broadcast_multiply_fusion.7) | copy-start | bytes 6148
  537.9 60.7 %copy-start.72 = (f32[512]{0:T(512)}, f32[512]{0:T(512)S(1)}, u32[]{:S(2)}) copy-start(f32[512]{0:T(512)S(1)} %fusion.384) | copy-start | bytes 6148
  537.9 60.7 %copy-start.90 = (f32[512]{0:T(512)}, f32[512]{0:T(512)S(1)}, u32[]{:S(2)}) copy-start(f32[512]{0:T(512)S(1)} %fusion.382) | copy-start | bytes 6148
  599.9 8.4 copy-start.11
  600.0 8.4 copy-start.76
  604.8 23.1 %all-to-all-start.8 = ((bf16[512,12,64]{0,2,1:T(8,128)(2,1)}), bf16[512,12,64]{0,2,1:T(8,128)(2,1)S(1)}, u32[]{:S(2)}, u32[]{:S(2)}) async-start(bf16[512,12,64]{0,2,1:T(8,128)(2,1)} %bitcast.66), calls=%async_computation.8 | async-start | bytes 1572864 | tf_op jit(solution)/shard_map/all_to_all | solution.py:256
  608.3 710.8 %reduce-scatter.13.cloned.1.call-start = ((), (), s32[]{:S(2)}) async-start(), calls=%async_computation.28 | async-start | bytes 2433024 | tf_op jit(solution)/shard_map/reduce_scatter | solution.py:327
  627.9 187.0 %all-to-all-start.12 = ((bf16[512,12,64]{0,2,1:T(8,128)(2,1)}), bf16[512,12,64]{0,2,1:T(8,128)(2,1)}, u32[]{:S(2)}, u32[]{:S(2)}) async-start(bf16[512,12,64]{0,2,1:T(8,128)(2,1)} %bitcast.104), calls=%async_computation.12 | async-start | bytes 1572864 | tf_op jit(solution)/shard_map/all_to_all | solution.py:256
  814.9 199.4 %all-to-all-start.11 = ((bf16[4,2,49152]{2,1,0:T(2,128)(2,1)}), bf16[4,2,49152]{2,1,0:T(2,128)(2,1)}, u32[]{:S(2)}, u32[]{:S(2)}) async-start(bf16[4,2,49152]{2,1,0:T(2,128)(2,1)} %reshape.1175), calls=%async_computation.11 | async-start | bytes 1572864 | tf_op jit(solution)/shard_map/all_to_all | solution.py:271
  1014.3 23.6 %all-to-all-start.15 = ((bf16[4,2,49152]{2,1,0:T(2,128)(2,1)}), bf16[4,2,49152]{2,1,0:T(2,128)(2,1)S(1)}, u32[]{:S(2)}, u32[]{:S(2)}) async-start(bf16[4,2,49152]{2,1,0:T(2,128)(2,1)} %reshape.1169), calls=%async_computation.15 | async-start | bytes 1572864 | tf_op jit(solution)/shard_map/all_to_all | solution.py:271
  1019.4 299.7 %reduce-scatter.23.cloned.1.call-start = ((), (), s32[]{:S(2)}) async-start(), calls=%async_computation.33 | async-start | bytes 2433024
  1059.2 23.9 %all-to-all-start.10 = ((bf16[4,2,49152]{2,1,0:T(2,128)(2,1)}), bf16[4,2,49152]{2,1,0:T(2,128)(2,1)}, u32[]{:S(2)}, u32[]{:S(2)}) async-start(bf16[4,2,49152]{2,1,0:T(2,128)(2,1)} %reshape.1171), calls=%async_computation.10 | async-start | bytes 1572864 | tf_op jit(solution)/shard_map/all_to_all | solution.py:268
  1083.1 29.6 %all-to-all-start.14 = ((bf16[4,2,49152]{2,1,0:T(2,128)(2,1)}), bf16[4,2,49152]{2,1,0:T(2,128)(2,1)}, u32[]{:S(2)}, u32[]{:S(2)}) async-start(bf16[4,2,49152]{2,1,0:T(2,128)(2,1)} %reshape.1165), calls=%async_computation.14 | async-start | bytes 1572864 | tf_op jit(solution)/shard_map/all_to_all | solution.py:268
  1087.3 231.7 %reduce-scatter.21.cloned.1.call-start = ((), (), s32[]{:S(2)}) async-start(), calls=%async_computation.32 | async-start | bytes 2433024
  1136.8 24.2 %all-to-all-start.9 = ((bf16[4,2,49152]{2,1,0:T(2,128)(2,1)}), bf16[4,2,49152]{2,1,0:T(2,128)(2,1)}, u32[]{:S(2)}, u32[]{:S(2)}) async-start(bf16[4,2,49152]{2,1,0:T(2,128)(2,1)} %reshape.1173), calls=%async_computation.9 | async-start | bytes 1572864 | tf_op jit(solution)/shard_map/all_to_all | solution.py:265
  1161.0 24.0 %all-to-all-start.13 = ((bf16[4,2,49152]{2,1,0:T(2,128)(2,1)}), bf16[4,2,49152]{2,1,0:T(2,128)(2,1)}, u32[]{:S(2)}, u32[]{:S(2)}) async-start(bf16[4,2,49152]{2,1,0:T(2,128)(2,1)} %reshape.1167), calls=%async_computation.13 | async-start | bytes 1572864 | tf_op jit(solution)/shard_map/all_to_all | solution.py:265
  1165.2 200.3 %reduce-scatter.19.cloned.1.call-start = ((), (), s32[]{:S(2)}) async-start(), calls=%async_computation.31 | async-start | bytes 2433024
  1200.7 306.5 %reduce-scatter.17.cloned.1.call-start = ((), (), s32[]{:S(2)}) async-start(), calls=%async_computation.30 | async-start | bytes 9732096 | tf_op jit(solution)/shard_map/reduce_scatter | solution.py:333
  1218.3 430.4 %reduce-scatter.15.cloned.1.call-start = ((), (), s32[]{:S(2)}) async-start(), calls=%async_computation.29 | async-start | bytes 9732096 | tf_op jit(solution)/shard_map/reduce_scatter | solution.py:331
  (154 other events, 483.9 us)
Sparse Core Ops, SparseCore 0:
  10.8 56.8 all-gather.8
  70.5 57.0 all-gather.6
  130.4 57.1 all-gather.10
  190.2 65.9 all-gather.12
  258.8 71.8 all-gather.14
  333.3 61.7 all-gather.16
  615.0 100.7 reduce-scatter.12
  1051.0 100.6 reduce-scatter.22
  1157.6 103.5 reduce-scatter.20
  1266.9 98.6 reduce-scatter.18
  1372.0 135.2 reduce-scatter.16
  1513.6 135.0 reduce-scatter.14
where the time goes:
time: 1670 us; the launch traced here: 1660 us
  waiting for transfers between devices  585 us (35%)
  matrix products  537 us (32%)
  local copies, waits for them, and re-layouts  221 us (13%)
  other arithmetic  86.3 us (5%)
  blocking collectives  81.3 us (5%)
  starting transfers between devices  69.6 us (4%)
  loops' own time  60.4 us (4%)
    reduce_scatter x1, waiting for transfers between devices, per_device(): lax.psum_scatter(totals[12], ('dp', 'seq'), scatter_dimension=0, tiled=True)  142 us
    reduce_scatter x1, waiting for transfers between devices, per_device(): lax.psum_scatter(totals[10], ('dp', 'seq'), scatter_dimension=0, tiled=True)  141 us
    dot_general x32, matrix products, attend(): jnp.einsum('igd,jgd->gij', query_sin, key_sin, precision=highest)  107 us
    dot_general x32, matrix products, attend(): scores = jnp.einsum('igd,jgd->gij', query_cos, key_cos, precision=highest)  99.1 us
    unnamed x237, local copies, waits for them, and re-layouts  89.4 us
    unnamed x2, blocking collectives  81.3 us
    dot_general x32, matrix products, attend(): numer = jnp.einsum('gij,jge->ige', scores, value_blk, precision=highest)  79.1 us
    another operation x4, loops' own time, attention(): final_state, outputs = lax.scan(jax.checkpoint(attend), initial, stacked)  60.4 us
  transfers between devices with their start and end apart: 28, of which 16 were waited for; matrix products, arithmetic and copies ran while one was open for 47% of the time, Pallas kernels for 0%

commit v1 on v0

v1 whole, which is shorter than its diff:
```python
import math

import jax
import jax.numpy as jnp
from jax import lax
from jax.experimental import pallas as pl
from jax.experimental.pallas import tpu as pltpu
from jax.sharding import PartitionSpec as P

H = 12
HD = 64
LANES = 128
NORM_EPS = 1e-05
HALF_TURN = math.pi / 2
STATE_ROWS = 72
GELU_A = 0.7978845608028654
GELU_B = 0.044715
BF = jnp.bfloat16
F32 = jnp.float32


def dot_nn(a, b):
    return lax.dot_general(a, b, (((1,), (0,)), ((), ())), preferred_element_type=F32)


def dot_nt(a, b):
    return lax.dot_general(a, b, (((1,), (1,)), ((), ())), preferred_element_type=F32)


def dot_tn(a, b):
    return lax.dot_general(a, b, (((0,), (0,)), ((), ())), preferred_element_type=F32)


def lane_first(shape):
    return lax.broadcasted_iota(jnp.int32, shape, 1) < HD


def pair_ones():
    row = lax.broadcasted_iota(jnp.int32, (LANES, LANES), 0) < HD
    col = lax.broadcasted_iota(jnp.int32, (LANES, LANES), 1) < HD
    return (row == col).astype(F32)


def head_sum(values, ones_low):
    high = values.astype(BF)
    rest = (values - high.astype(F32)).astype(BF)
    return dot_nn(jnp.concatenate([high, rest], axis=1), jnp.concatenate([ones_low, ones_low], axis=0))


def spread_state(packed):
    first = lane_first((HD, LANES))
    zero = jnp.zeros_like(packed)
    return jnp.concatenate(
        [jnp.where(first, packed, zero), jnp.where(first, zero, packed)], axis=0
    ).astype(BF)


def pack_state(full, row):
    first = lane_first((HD, LANES))
    packed = jnp.where(first, full[:HD], full[HD:])
    tail = jnp.concatenate([row, jnp.zeros((STATE_ROWS - HD - 1, LANES), F32)], axis=0)
    return jnp.concatenate([packed, tail], axis=0)


def key_state_kernel(k_ref, v_ref, cos_ref, sin_ref, out_ref):
    keys = jnp.maximum(k_ref[...], 0)
    vals = v_ref[...].astype(F32)
    cos, sin = cos_ref[...], sin_ref[...]
    both = jnp.concatenate([(vals * cos).astype(BF), (vals * sin).astype(BF)], axis=1)
    full = dot_tn(keys, both)
    keys32 = keys.astype(F32)
    row_cos = jnp.sum(keys32 * cos, axis=0, keepdims=True)
    row_sin = jnp.sum(keys32 * sin, axis=0, keepdims=True)
    out_ref[0, 0] = pack_state(full[:, :LANES], row_cos).astype(BF)
    out_ref[0, 1] = pack_state(full[:, LANES:], row_sin).astype(BF)


def tile_rows(rows):
    return min(256, rows)


def mix_kernel(q_ref, k_ref, v_ref, b_ref, w_ref, cos_ref, sin_ref, st_ref, mixed_ref, out_ref, den_ref):
    rows = q_ref.shape[0]
    tile = tile_rows(rows)
    ones_pair = pair_ones().astype(BF)
    keys = jnp.maximum(k_ref[...], 0)
    vals = jnp.concatenate([v_ref[...], jnp.ones((rows, LANES), BF)], axis=1)
    states = jnp.concatenate(
        [spread_state(st_ref[0, 0, :HD]), spread_state(st_ref[0, 1, :HD])], axis=1
    )
    row_cos, row_sin = st_ref[0, 0, HD : HD + 1], st_ref[0, 1, HD : HD + 1]
    first = lane_first((tile, LANES))
    for step in range(rows // tile):
        at = slice(step * tile, (step + 1) * tile)
        seen = (step + 1) * tile
        query = jnp.maximum(q_ref[at], 0)
        cos, sin = cos_ref[at], sin_ref[at]
        zero = jnp.zeros_like(query)
        weight = w_ref[0, at, :seen]
        heads = []
        for own in (jnp.where(first, query, zero), jnp.where(first, zero, query)):
            scores = dot_nt(own, keys[:seen]) * weight
            heads.append(dot_nn(scores.astype(BF), vals[:seen]))
        num = jnp.where(first, heads[0][:, :LANES], heads[1][:, :LANES])
        den = jnp.where(first, heads[0][:, LANES:], heads[1][:, LANES:])
        past = dot_nn(query, states)
        num = num + cos * past[:, :LANES] + sin * past[:, LANES:]
        den = den + head_sum(query.astype(F32) * (cos * row_cos + sin * row_sin), ones_pair)
        out = (num + den * b_ref[...]) / jnp.maximum(den, 1.0)
        mixed_ref[at] = out.astype(BF)
        out_ref[at] = out
        den_ref[at] = den


def mix_grads(d_out, out, den, bias, ones_pair):
    inverse = 1.0 / jnp.maximum(den, 1.0)
    d_num = (d_out.astype(F32) * inverse).astype(BF)
    gate = jnp.where(den > 1.0, 1.0, jnp.where(den == 1.0, 0.5, 0.0))
    return d_num, head_sum(d_num.astype(F32) * (bias - out * gate), ones_pair)


def query_state_kernel(q_ref, d_ref, out_ref, den_ref, b_ref, cos_ref, sin_ref, st_ref):
    ones_pair = pair_ones().astype(BF)
    query = jnp.maximum(q_ref[...], 0)
    cos, sin = cos_ref[...], sin_ref[...]
    d_num, d_den = mix_grads(d_ref[...], out_ref[...], den_ref[...], b_ref[...], ones_pair)
    d_num32 = d_num.astype(F32)
    both = jnp.concatenate([(d_num32 * cos).astype(BF), (d_num32 * sin).astype(BF)], axis=1)
    full = dot_tn(query, both)
    part = query.astype(F32) * d_den
    st_ref[0, 0] = pack_state(full[:, :LANES], jnp.sum(part * cos, axis=0, keepdims=True)).astype(BF)
    st_ref[0, 1] = pack_state(full[:, LANES:], jnp.sum(part * sin, axis=0, keepdims=True)).astype(BF)


def mix_back_kernel(
    q_ref, k_ref, v_ref, d_ref, out_ref, den_ref, b_ref, low_ref, up_ref, cos_ref, sin_ref, past_ref, next_ref,
    dq_ref, dk_ref, dv_ref,
):
    rows = q_ref.shape[0]
    tile = tile_rows(rows)
    ones_pair = pair_ones().astype(BF)
    first = lane_first((rows, LANES))
    lane = lax.broadcasted_iota(jnp.int32, (rows, LANES), 1)
    query = jnp.maximum(q_ref[...], 0)
    keys = jnp.maximum(k_ref[...], 0)
    vals = v_ref[...]
    cos, sin = cos_ref[...], sin_ref[...]
    d_num, d_den = mix_grads(d_ref[...], out_ref[...], den_ref[...], b_ref[...], ones_pair)
    high = d_den.astype(BF)
    rest = (d_den - high.astype(F32)).astype(BF)
    zero = jnp.zeros((rows, LANES), BF)
    spot = lane % HD
    marks = jnp.where(spot == 0, high, jnp.where(spot == 1, rest, zero))
    vals_one = jnp.concatenate([vals, jnp.ones((rows, LANES), BF)], axis=1)

    past = [spread_state(past_ref[0, i, :HD]) for i in range(2)]
    past_row = [past_ref[0, i, HD : HD + 1] for i in range(2)]
    d_query = cos * dot_nt(d_num, past[0]) + sin * dot_nt(d_num, past[1])
    d_query = d_query + d_den * (cos * past_row[0] + sin * past_row[1])
    later = [spread_state(next_ref[0, i, :HD]) for i in range(2)]
    later_row = [next_ref[0, i, HD : HD + 1] for i in range(2)]
    d_keys = cos * (dot_nt(vals, later[0]) + later_row[0]) + sin * (dot_nt(vals, later[1]) + later_row[1])
    from_keys = dot_nn(keys, jnp.concatenate(later, axis=1))
    d_vals = cos * from_keys[:, :LANES] + sin * from_keys[:, LANES:]

    own_query = (jnp.where(first, query, zero), jnp.where(first, zero, query))
    own_d = tuple(
        jnp.concatenate([jnp.where(pick, d_num, zero), jnp.where(pick, marks, zero)], axis=1)
        for pick in (first, jnp.logical_not(first))
    )
    for step in range(rows // tile):
        at = slice(step * tile, (step + 1) * tile)
        seen = (step + 1) * tile
        some = first[at]
        parts = []
        for one in range(2):
            d_scores = dot_nt(own_d[one][at], vals_one[:seen]) * low_ref[0, at, :seen]
            parts.append(dot_nn(d_scores.astype(BF), keys[:seen]))
        total = d_query[at] + jnp.where(some, parts[0], parts[1])
        dq_ref[at] = jnp.where(q_ref[at] > 0, total, 0.0).astype(BF)
        onward = slice(step * tile, rows)
        weight = up_ref[0, at, onward]
        key_parts, val_parts = [], []
        for one in range(2):
            scores = dot_nt(keys[at], own_query[one][onward]) * weight
            val_parts.append(dot_nn(scores.astype(BF), d_num[onward]))
            d_scores = dot_nt(vals_one[at], own_d[one][onward]) * weight
            key_parts.append(dot_nn(d_scores.astype(BF), query[onward]))
        total = d_keys[at] + jnp.where(some, key_parts[0], key_parts[1])
        dk_ref[at] = jnp.where(k_ref[at] > 0, total, 0.0).astype(BF)
        dv_ref[at] = (d_vals[at] + jnp.where(some, val_parts[0], val_parts[1])).astype(BF)


class Mixer:
    def __init__(self, count, rows, width):
        self.count, self.rows, self.width = count, rows, width
        self.pairs = width // LANES

    def wide(self, group=0):
        offset = group * self.pairs
        return pl.BlockSpec((self.rows, LANES), lambda m, p: (m, offset + p))

    def angle(self):
        return pl.BlockSpec((self.rows, LANES), lambda m, p: (m, 0))

    def bias(self):
        return pl.BlockSpec((1, LANES), lambda m, p: (0, p))

    def state(self):
        return pl.BlockSpec((1, 2, STATE_ROWS, LANES), lambda m, p: (m, 0, 0, p))

    def square(self):
        return pl.BlockSpec((1, self.rows, self.rows), lambda m, p: (m, 0, 0))

    def state_shape(self):
        return jax.ShapeDtypeStruct((self.count, 2, STATE_ROWS, self.width), BF)

    def flat_shape(self, dtype):
        return jax.ShapeDtypeStruct((self.count * self.rows, self.width), dtype)

    def call(self, kernel, in_specs, out_specs, out_shape, flops):
        return pl.pallas_call(
            kernel,
            grid=(self.count, self.pairs),
            in_specs=in_specs,
            out_specs=out_specs,
            out_shape=out_shape,
            cost_estimate=pl.CostEstimate(
                flops=flops * self.count * self.pairs, bytes_accessed=1 << 23, transcendentals=0
            ),
        )

    def key_states(self, qkv, cos, sin):
        flops = 4 * self.rows * LANES * LANES
        return self.call(
            key_state_kernel,
            [self.wide(1), self.wide(2), self.angle(), self.angle()],
            self.state(),
            self.state_shape(),
            flops,
        )(qkv, qkv, cos, sin)

    def mix(self, qkv, bias, low, cos, sin, past):
        flops = 12 * self.rows * self.rows * LANES
        return self.call(
            mix_kernel,
            [self.wide(0), self.wide(1), self.wide(2), self.bias(), self.square(), self.angle(), self.angle(), self.state()],
            [self.wide()] * 3,
            [self.flat_shape(BF), self.flat_shape(F32), self.flat_shape(F32)],
            flops,
        )(qkv, qkv, qkv, bias, low, cos, sin, past)

    def query_states(self, qkv, d_mixed, out, den, bias, cos, sin):
        flops = 4 * self.rows * LANES * LANES
        return self.call(
            query_state_kernel,
            [self.wide(0)] + [self.wide()] * 3 + [self.bias()] + [self.angle()] * 2,
            self.state(),
            self.state_shape(),
            flops,
        )(qkv, d_mixed, out, den, bias, cos, sin)

    def mix_back(self, qkv, d_mixed, out, den, bias, low, up, cos, sin, past, later):
        flops = 30 * self.rows * self.rows * LANES
        return self.call(
            mix_back_kernel,
            [self.wide(0), self.wide(1), self.wide(2)]
            + [self.wide()] * 3
            + [self.bias()]
            + [self.square()] * 2
            + [self.angle()] * 2
            + [self.state()] * 2,
            [self.wide()] * 3,
            [self.flat_shape(BF)] * 3,
            flops,
        )(qkv, qkv, qkv, d_mixed, out, den, bias, low, up, cos, sin, past, later)


def outside_sum(state, forward):
    size = lax.axis_size("seq")

    def shift(values, distance):
        if forward:
            pairs = [(i, i + distance) for i in range(size - distance)]
        else:
            pairs = [(i + distance, i) for i in range(size - distance)]
        return lax.ppermute(values, "seq", pairs)

    moved = shift(state, 1)
    total = moved.astype(F32)
    reach = 1
    while reach + 1 < size:
        span = min(reach + 1, size - 1 - reach)
        block = (state.astype(F32) + total).astype(BF)
        if span < reach + 1:
            raise NotImplementedError
        got = shift(block, span)
        total = total + got.astype(F32)
        reach = reach + span
    return total


def swap(values, bit):
    size = lax.axis_size("dp")
    return lax.ppermute(values, "dp", [(i, i ^ (1 << bit)) for i in range(size)])


def scatter_sum(pieces):
    dp_size, seq_size, rows, width = pieces.shape
    bits = dp_size.bit_length() - 1
    place = lax.axis_index("dp")

    def fold(values, axis, bit):
        mine = (place >> bit) & 1
        kept = lax.dynamic_index_in_dim(values, mine, axis, keepdims=False)
        sent = lax.dynamic_index_in_dim(values, 1 - mine, axis, keepdims=False)
        return (kept.astype(F32) + swap(sent.astype(BF), bit).astype(F32)).astype(BF)

    values = pieces.reshape((2,) * bits + (seq_size, rows, width))
    values = fold(values, bits - 1, 0)
    half = (bits - 1) // 2
    others = list(range(1, bits))
    orders = (others[:half] + others[half:], others[half:] + others[:half])
    cut = (rows // 2 + 7) // 8 * 8
    z = lax.axis_index("seq")
    results = []
    for order, span in zip(orders, (slice(0, cut), slice(cut, rows))):
        part = values[..., span, :]
        left = list(others)
        for bit in order:
            axis = [b for b in sorted(left, reverse=True)].index(bit)
            part = fold(part, axis, bit)
            left.remove(bit)
        total = lax.dynamic_index_in_dim(part, z, 0, keepdims=False).astype(F32)
        for distance in range(1, seq_size):
            sent = lax.dynamic_index_in_dim(part, (z + distance) % seq_size, 0, keepdims=False)
            got = lax.ppermute(sent, "seq", [(i, (i + distance) % seq_size) for i in range(seq_size)])
            total = total + got.astype(F32)
        results.append(total)
    return jnp.concatenate(results, axis=0)


def norm_stats(values):
    center = values - jnp.mean(values, axis=-1, keepdims=True)
    spread = jnp.mean(center * center, axis=-1, keepdims=True)
    scale = lax.rsqrt(spread + NORM_EPS)
    return center * scale, scale


def norm_back(grad, normed, scale, gain):
    inner = grad * gain
    return scale * (
        inner
        - jnp.mean(inner, axis=-1, keepdims=True)
        - normed * jnp.mean(inner * normed, axis=-1, keepdims=True)
    )


def per_device(
    tokens,
    seq_lengths,
    query_weight,
    query_bias,
    key_weight,
    key_bias,
    value_weight,
    value_bias,
    output_weight,
    output_bias,
    gain_first,
    shift_first,
    inner_weight,
    inner_bias,
    outer_weight,
    outer_bias,
    gain_second,
    shift_second,
    cotangent,
):
    dp_size, seq_size = lax.axis_size("dp"), lax.axis_size("seq")
    owners = dp_size * seq_size
    micro_count, seqs_here, shard_rows, width = tokens.shape
    count = micro_count * seqs_here
    total = count * shard_rows
    share = query_weight.shape[0]
    hidden_width = inner_weight.shape[1]
    fan = hidden_width // width
    seq_place = lax.axis_index("seq")
    mixer = Mixer(count, shard_rows, width)

    vectors = [query_bias, key_bias, value_bias, output_bias, gain_first, shift_first, outer_bias, gain_second, shift_second]
    vector_row = jnp.concatenate(vectors + [inner_bias])
    vector_fill = width - vector_row.shape[0]
    vector_block = jnp.pad(vector_row[None, :], ((0, 7), (0, vector_fill)))
    head_rows = jnp.concatenate([vector_block, query_weight, key_weight, value_weight], axis=0)
    tail_rows = jnp.concatenate(
        [output_weight] + [inner_weight[:, i * width : (i + 1) * width] for i in range(fan)] + [outer_weight], axis=0
    )
    head_all = lax.all_gather(head_rows, ("dp", "seq"), axis=0)
    tail_all = lax.all_gather(tail_rows, ("dp", "seq"), axis=0)

    vec = head_all[:, 0, :].astype(F32)
    (b_query, b_key, b_value, b_output, gain_one, shift_one, b_outer, gain_two, shift_two) = (
        vec[:, i * share : (i + 1) * share].reshape(width) for i in range(9)
    )
    b_inner = vec[:, 9 * share : 9 * share + hidden_width // owners].reshape(hidden_width)
    w_qkv = jnp.concatenate(
        [head_all[:, 8 + i * share : 8 + (i + 1) * share].reshape(width, width) for i in range(3)], axis=1
    )
    b_qkv = jnp.concatenate([b_query, b_key, jnp.zeros((width,), F32)])
    bias_row = b_value[None, :]
    w_output = tail_all[:, :share].reshape(width, width)
    w_inner = jnp.concatenate(
        [tail_all[:, (1 + i) * share : (2 + i) * share].reshape(width, width) for i in range(fan)], axis=1
    )
    w_outer = tail_all[:, (1 + fan) * share :].reshape(hidden_width, width)

    limit = seq_lengths.reshape(count).astype(F32)
    places = (seq_place * shard_rows + jnp.arange(shard_rows)).astype(F32)
    angle = HALF_TURN * places[None, :] / limit[:, None]
    live = (places[None, :] < limit[:, None]).astype(F32)
    cos, sin = jnp.cos(angle) * live, jnp.sin(angle) * live
    square = cos[:, :, None] * cos[:, None, :] + sin[:, :, None] * sin[:, None, :]
    causal = jnp.tril(jnp.ones((shard_rows, shard_rows), F32))
    low, up = square * causal, square * causal.T
    cos = jnp.broadcast_to(cos.reshape(total, 1), (total, LANES))
    sin = jnp.broadcast_to(sin.reshape(total, 1), (total, LANES))

    x_low = tokens.reshape(total, width)
    qkv = (dot_nn(x_low, w_qkv) + b_qkv).astype(BF)
    states = mixer.key_states(qkv, cos, sin)
    past = outside_sum(states, True)
    mixed, mixed_full, den = mixer.mix(qkv, bias_row, low, cos, sin, past)

    resid_one = x_low.astype(F32) + (dot_nn(mixed, w_output) + b_output)
    norm_one, scale_one = norm_stats(resid_one)
    first = norm_one * gain_one + shift_one
    first_low = first.astype(BF)
    inner = dot_nn(first_low, w_inner) + b_inner
    bent = jnp.tanh(GELU_A * (inner + GELU_B * inner * inner * inner))
    hidden = (0.5 * inner * (1.0 + bent)).astype(BF)
    outer = dot_nn(hidden, w_outer) + b_outer
    norm_two, scale_two = norm_stats(first + outer)
    layer_out = (norm_two * gain_two + shift_two).astype(BF)

    grad_final = cotangent.reshape(total, width).astype(F32)
    grad_gain_two = jnp.sum(grad_final * norm_two, axis=0)
    grad_shift_two = jnp.sum(grad_final, axis=0)
    d_second = norm_back(grad_final, norm_two, scale_two, gain_two)
    d_outer = d_second.astype(BF)
    grad_w_outer = dot_tn(hidden, d_outer)
    grad_b_outer = jnp.sum(d_outer.astype(F32), axis=0)
    d_hidden = dot_nt(d_outer, w_outer)
    slope = 0.5 * (1.0 + bent) + 0.5 * inner * (1.0 - bent * bent) * GELU_A * (1.0 + 3.0 * GELU_B * inner * inner)
    d_inner = (d_hidden * slope).astype(BF)
    grad_w_inner = dot_tn(first_low, d_inner)
    grad_b_inner = jnp.sum(d_inner.astype(F32), axis=0)
    d_first = d_second + dot_nt(d_inner, w_inner)
    grad_gain_one = jnp.sum(d_first * norm_one, axis=0)
    grad_shift_one = jnp.sum(d_first, axis=0)
    d_resid = norm_back(d_first, norm_one, scale_one, gain_one)
    d_attended = d_resid.astype(BF)
    grad_w_output = dot_tn(mixed, d_attended)
    grad_b_output = jnp.sum(d_attended.astype(F32), axis=0)
    d_mixed = dot_nt(d_attended, w_output).astype(BF)

    def owned(grad):
        return grad.astype(BF).reshape(dp_size, seq_size, grad.shape[0] // owners, width)

    tail_grads = [owned(grad_w_output)]
    tail_grads += [owned(grad_w_inner[:, i * width : (i + 1) * width]) for i in range(fan)]
    tail_sum = scatter_sum(jnp.concatenate(tail_grads + [owned(grad_w_outer)], axis=2))

    d_states = mixer.query_states(qkv, d_mixed, mixed_full, den, bias_row, cos, sin)
    later = outside_sum(d_states, False)
    d_query, d_key, d_value = mixer.mix_back(qkv, d_mixed, mixed_full, den, bias_row, low, up, cos, sin, past, later)
    d_three = (d_query, d_key, d_value)
    grad_w = [dot_tn(x_low, d) for d in d_three]
    grad_b = [jnp.sum(d.astype(F32), axis=0) for d in d_three]
    d_tokens = d_resid
    for i, d in enumerate(d_three):
        d_tokens = d_tokens + dot_nt(d, w_qkv[:, i * width : (i + 1) * width])

    vec_grads = grad_b + [grad_b_output, grad_gain_one, grad_shift_one, grad_b_outer, grad_gain_two, grad_shift_two]
    vec_rows = jnp.concatenate(
        [g.reshape(owners, share) for g in vec_grads] + [grad_b_inner.reshape(owners, hidden_width // owners)], axis=1
    )
    vec_rows = jnp.pad(vec_rows[:, None, :], ((0, 0), (0, 7), (0, vector_fill)))
    vec_rows = vec_rows.reshape(dp_size, seq_size, 8, width).astype(BF)
    head_sum_rows = scatter_sum(jnp.concatenate([vec_rows] + [owned(g) for g in grad_w], axis=2))

    vec_out = head_sum_rows[0]
    out_vec = [vec_out[i * share : (i + 1) * share] for i in range(9)]
    out_b_inner = vec_out[9 * share : 9 * share + hidden_width // owners]
    out_w = [head_sum_rows[8 + i * share : 8 + (i + 1) * share] for i in range(3)]
    out_w_output = tail_sum[:share]
    out_w_inner = jnp.concatenate([tail_sum[(1 + i) * share : (2 + i) * share] for i in range(fan)], axis=1)
    out_w_outer = tail_sum[(1 + fan) * share :]
    return (
        layer_out.reshape(tokens.shape),
        d_tokens.reshape(tokens.shape),
        out_w[0],
        out_vec[0],
        out_w[1],
        out_vec[1],
        out_w[2],
        out_vec[2],
        out_w_output,
        out_vec[3],
        out_vec[4],
        out_vec[5],
        out_w_inner,
        out_b_inner,
        out_w_outer,
        out_vec[6],
        out_vec[7],
        out_vec[8],
    )


def solution(mesh):
    rows = P(("dp", "seq"), None)
    vector = P(("dp", "seq"))
    act = P(None, "dp", "seq", None)
    layer = (rows, vector) * 4 + (vector, vector) + (rows, vector) * 2 + (vector, vector)
    return jax.shard_map(
        per_device,
        mesh=mesh,
        in_specs=(act, P(None, "dp")) + layer + (act,),
        out_specs=(act, act) + layer,
        check_vma=False,
    )
```

time: 1670 us -> 495 us (0.30)
  matrix products: 537 us -> 95.7 us
  waiting for transfers between devices: 585 us -> 184 us
  local copies, waits for them, and re-layouts: 221 us -> 56.9 us
  blocking collectives: 81.3 us -> 0 us
  Pallas kernels: 0 us -> 66.8 us
  loops' own time: 60.4 us -> 0 us
  other arithmetic: 86.3 us -> 35.1 us
  starting transfers between devices: 69.6 us -> 35.6 us
    dot_general x292 -> x16, matrix products: 537 us -> 95.7 us  [the longest x6 35.2 us: dot_nt(): lax.dot_general(a, b, (((1,), (1,)), ((), ())), preferred_element_type=F32)]
    reduce_scatter x3 -> x0, waiting for transfers between devices: 283 us -> none  [the longest x1 142 us: per_device(): lax.psum_scatter(totals[12], ('dp', 'seq'), scatter_dimension=0, tiled=True)]
    all_to_all x16 -> x0, waiting for transfers between devices: 139 us -> none  [the longest x2 28.8 us: per_device(): lax.all_to_all(d_key_heads.astype(jnp.bfloat16), 'seq', split_axis=0, con...]
    ppermute x0 -> x26, waiting for transfers between devices: none -> 101 us  [the longest x10 41.8 us: swap(): return lax.ppermute(values, 'dp', [(i, i ^ 1 << bit) for i in range(size)])]
    unnamed x2 -> x0, blocking collectives: 81.3 us -> none
    unnamed x237 -> x77, local copies, waits for them, and re-layouts: 89.4 us -> 15.3 us
    all_to_all x16 -> x0, starting transfers between devices: 69.1 us -> none  [the longest x2 10.9 us: per_device(): lax.all_to_all(mixed_send, 'seq', split_axis=0, concat_axis=1, tiled=True)]
    pallas_call x0 -> x4, Pallas kernels: none -> 66.8 us  [the longest x1 30.5 us: mix_back(): self.call(mix_back_kernel, [self.wide(0), self.wide(1), self.wide(2)] + [...]
  transfers between devices with their start and end apart: 28 -> 28, of which waited for: 16 -> 18; matrix products, arithmetic and copies ran while one was open for 47% -> 19% of each run, Pallas kernels for 0% -> 11%
where the time goes in v1:
time: 495 us; the launch traced here: 489 us
  waiting for transfers between devices  184 us (37%)
  matrix products  95.7 us (19%)
  Pallas kernels  66.8 us (13%)
  local copies, waits for them, and re-layouts  56.9 us (11%)
  starting transfers between devices  35.6 us (7%)
  other arithmetic  35.1 us (7%)
  between operations  15.1 us (3%)
    all_gather x1, waiting for transfers between devices, per_device(): head_all = lax.all_gather(head_rows, ('dp', 'seq'), axis=0)  57.4 us
    ppermute x10, waiting for transfers between devices, swap(): return lax.ppermute(values, 'dp', [(i, i ^ 1 << bit) for i in range(size)])  41.8 us
    dot_general x6, matrix products, dot_nt(): lax.dot_general(a, b, (((1,), (1,)), ((), ())), preferred_element_type=F32)  35.2 us
    dot_general x6, matrix products, dot_tn(): lax.dot_general(a, b, (((0,), (0,)), ((), ())), preferred_element_type=F32)  32.4 us
    ppermute x4, waiting for transfers between devices, shift(): return lax.ppermute(values, 'seq', pairs)  31.8 us
    pallas_call x1, Pallas kernels, mix_back(): self.call(mix_back_kernel, [self.wide(0), self.wide(1), self.wide(2)] + [...  30.5 us
    dot_general x4, matrix products, dot_nn(): lax.dot_general(a, b, (((1,), (0,)), ((), ())), preferred_element_type=F32)  28.1 us
    ppermute x12, waiting for transfers between devices, scatter_sum(): lax.ppermute(sent, 'seq', [(i, (i + distance) % seq_size) for i in range(...  27.5 us
  transfers between devices with their start and end apart: 28, of which 18 were waited for; matrix products, arithmetic and copies ran while one was open for 19% of the time, Pallas kernels for 11%

profile of v1, /device:TPU:0, one launch (start us, length us, event | category | flops | bytes accessed | tf_op | source)
XLA Modules:
  0.0 489.0 jit_solution(18056206872210551636)
XLA Ops:
  7.2 6.8 %concatenate.57 = bf16[312]{0:T(512)(128)(2,1)S(1)} concatenate(bf16[24]{0:T(256)(128)(2,1)} %param.22, bf16[24]{0:T(256)(128)(2,1)} %param.24, bf16[24]{0:T(256)(128)(2,1)} %param.26, bf16[24]{0:T(256)(128)(2,1)} %param.28, bf16[24]{0:T(256)(128)(2,1)} %param.29, bf16[24]{0:T(256)(128)(2,1)} %param.30, bf16[24]{0:T(256)(128)(2,1)} %param.34, bf16[24]{0:T(256)(128)(2,1)} %param.35, ...), dimensions={0} | concatenate | bytes 1248 | tf_op jit(solution)/shard_map/concatenate | solution.py:392
  21.9 57.4 %all-gather.5.cloned.1.call-done = bf16[2560,768]{1,0:T(8,128)(2,1)} async-done(((bf16[80,768]{1,0:T(8,128)(2,1)}), bf16[2560,768]{1,0:T(8,128)(2,1)}) %all-gather.5.cloned.1.call-update) | async-done | bytes 3932176 | tf_op jit(solution)/shard_map/all_gather | solution.py:399
  80.7 2.3 fusion.64
  83.2 6.1 %fusion.8.k_ref.v_ref.q_ref = bf16[1024,2304]{1,0:T(8,128)(2,1)} fusion(bf16[1024,768]{1,0:T(8,128)(2,1)S(1)} %bitcast.242, f32[2304]{0:T(1024)S(1)} %pad_maximum_fusion.6, bf16[768,768]{1,0:T(8,128)(2,1)S(1)} %bitcast.210, bf16[768,768]{1,0:T(8,128)(2,1)S(1)} %bitcast.229, bf16[768,768]{1,0:T(8,128)(2,1)S(1)} %bitcast.227), kind=kOutput, calls=%fused_computation.16 | convolution fusion | flops 3639214080 | bytes 9839616 | tf_op jit(solution)/shard_map/dot_general | solution.py:23
  91.3 9.2 %shard_map.322 = bf16[2,2,72,768]{3,2,1,0:T(8,128)(2,1)} custom-call(bf16[1024,2304]{1,0:T(8,128)(2,1)} %fusion.8.k_ref.v_ref.q_ref, bf16[1024,2304]{1,0:T(8,128)(2,1)} %fusion.8.k_ref.v_ref.q_ref, f32[1024,128]{1,0:T(8,128)} %broadcast_in_dim.21.cos_ref, f32[1024,128]{1,0:T(8,128)} %broadcast_in_dim.22.sin_ref), custom_call_target="tpu_custom_call" | custom-call | flops 402653184 | bytes 8388608 | tf_op jit(solution)/shard_map/pallas_call | solution.py:235
  100.5 3.1 collective-permute-start
  103.9 15.9 %collective-permute-done = bf16[2,2,72,768]{3,2,1,0:T(8,128)(2,1)S(1)} collective-permute-done((bf16[2,2,72,768]{3,2,1,0:T(8,128)(2,1)}, bf16[2,2,72,768]{3,2,1,0:T(8,128)(2,1)S(1)}, u32[]{:S(2)}, u32[]{:S(2)}) %collective-permute-start) | collective-permute-done | bytes 442400 | tf_op jit(solution)/shard_map/ppermute | solution.py:287
  120.9 8.3 %collective-permute-start.1 = (bf16[2,2,72,768]{3,2,1,0:T(8,128)(2,1)S(1)}, bf16[2,2,72,768]{3,2,1,0:T(8,128)(2,1)S(1)}, u32[]{:S(2)}, u32[]{:S(2)}) collective-permute-start(bf16[2,2,72,768]{3,2,1,0:T(8,128)(2,1)S(1)} %fusion.33), channel_id=1, source_target_pairs={{0,2},{1,3},{4,6},{5,7},{8,10},{9,11},{12,14},{13,15},{16,18},{17,... | collective-permute-start | bytes 1327112 | tf_op jit(solution)/shard_map/ppermute | solution.py:287
  129.3 2.6 fusion.25
  134.6 2.8 collective-permute-done.1
  138.4 16.4 %shard_map.323 = (bf16[1024,768]{1,0:T(8,128)(2,1)}, f32[1024,768]{1,0:T(8,128)}, f32[1024,768]{1,0:T(8,128)}) custom-call(bf16[1024,2304]{1,0:T(8,128)(2,1)} %fusion.8.k_ref.v_ref.q_ref, bf16[1024,2304]{1,0:T(8,128)(2,1)} %fusion.8.k_ref.v_ref.q_ref, bf16[1024,2304]{1,0:T(8,128)(2,1)} %fusion.8.k_ref.v_ref.q_ref, f32[1,768]{1,0:T(1,128)} %broadcast_in_dim_reshape.2.b_ref, ...), custom_call_target="tpu_custom_call" | custom-call | flops 4831838208 | bytes 8388608 | tf_op jit(solution)/shard_map/pallas_call | solution.py:245
  154.8 25.4 %all-gather.7.cloned.1.call-done = bf16[6912,768]{1,0:T(8,128)(2,1)} async-done(((bf16[216,768]{1,0:T(8,128)(2,1)}), bf16[6912,768]{1,0:T(8,128)(2,1)}) %all-gather.7.cloned.1.call-update) | async-done | bytes 10616848 | tf_op jit(solution)/shard_map/all_gather | solution.py:400
  180.1 2.6 slice.275
  182.8 3.2 fusion.62
  188.6 9.7 %fusion.35 = f32[1024,3072]{1,0:T(8,128)} fusion(bf16[768,768]{1,0:T(8,128)(2,1)S(1)} %bitcast.221, bf16[768,768]{1,0:T(8,128)(2,1)S(1)} %bitcast.223, bf16[768,768]{1,0:T(8,128)(2,1)S(1)} %bitcast.225, bf16[768,768]{1,0:T(8,128)(2,1)S(1)} %bitcast.219, f32[1024,768]{1,0:T(8,128)S(1)} %get-tuple-element.153, f32[768]{0:T(1024)S(1)} %add.324, ...), kind=kOutput, calls=%fused_computation.85 | convolution fusion | flops 4854644736 | bytes 20461568 | tf_op jit(solution)/shard_map/dot_general | solution.py:23
  198.3 10.7 %fusion.70 = (f32[1024]{0:T(1024)S(1)}, f32[1024,768]{1,0:T(8,128)S(1)}) fusion(f32[768]{0:T(1024)S(1)} %add.332, bf16[3072,768]{1,0:T(8,128)(2,1)S(1)} %bitcast.208, f32[1024,3072]{1,0:T(8,128)} %fusion.35, f32[3072]{0:T(1024)S(1)} %add.327, f32[768]{0:T(1024)S(1)} %add.324, f32[768]{0:T(1024)S(1)} %mul.232, f32[1024]{0:T(1024)S(1)} %add_rsqrt_fusion.1, ...), kind=kOutput, calls=%fused_computation.186 | convolution fusion | flops 4868799488 | bytes 23626752 | tf_op jit(solution)/shard_map/dot_general | solution.py:23
  209.5 2.7 fusion.21
  213.5 16.0 %fusion.71 = (bf16[3072]{0:T(1024)(128)(2,1)S(1)}, bf16[1024,3072]{1,0:T(8,128)(2,1)}) fusion(f32[1024,3072]{1,0:T(8,128)} %fusion.35, f32[3072]{0:T(1024)S(1)} %add.327, bf16[3072,768]{1,0:T(8,128)(2,1)S(1)} %bitcast.209, f32[1024,768]{1,0:T(8,128)S(1)} %get-tuple-element.91), kind=kOutput, calls=%fused_computation.187 | convolution fusion | flops 4898681856 | bytes 26757120 | tf_op jit(solution)/shard_map/dot_general | solution.py:27
  229.4 8.8 %multiply_reduce_fusion = (bf16[768]{0:T(1024)(128)(2,1)S(1)}, f32[1024]{0:T(1024)S(1)}, f32[1024]{0:T(1024)S(1)}, bf16[768]{0:T(1024)(128)(2,1)S(1)}, f32[1024,768]{1,0:T(8,128)S(1)}) fusion(f32[1024,768]{1,0:T(8,128)S(1)} %get-tuple-element.153, f32[1024]{0:T(1024)S(1)} %add_rsqrt_fusion.1, f32[1024]{0:T(1024)S(1)} %broadcast_multiply_fusion.4, ...), kind=kOutput, calls=%fused_computation.36 | convolution fusion | flops 4858572800 | bytes 20469760 | tf_op jit(solution)/shard_map/dot_general | solution.py:27
  239.6 2.6 convolution_convert_fusion.2.d_ref
  242.2 2.5 convolution_convert_fusion.3
  244.7 8.1 %convolution_convert_fusion.1 = bf16[768,3072]{1,0:T(8,128)(2,1)} fusion(bf16[1024,3072]{1,0:T(8,128)(2,1)S(1)} %bitcast.247, f32[1024,768]{1,0:T(8,128)S(1)} %get-tuple-element.153, f32[768]{0:T(1024)S(1)} %add.324, f32[768]{0:T(1024)S(1)} %mul.232, f32[1024]{0:T(1024)S(1)} %add_rsqrt_fusion.1, f32[1024]{0:T(1024)S(1)} %broadcast_multiply_fusion.4), kind=kOutput, calls=%fused_computation.15 | convolution fusion | flops 4838129664 | bytes 14170112 | tf_op jit(solution)/shard_map/dot_general | solution.py:31
  252.8 12.2 %convolution_convert_fusion = bf16[3072,768]{1,0:T(8,128)(2,1)} fusion(f32[1024,768]{1,0:T(8,128)S(1)} %get-tuple-element.91, f32[1024,3072]{1,0:T(8,128)} %fusion.35, f32[3072]{0:T(1024)S(1)} %add.327), kind=kOutput, calls=%fused_computation.14 | convolution fusion | flops 4866441216 | bytes 20459520 | tf_op jit(solution)/shard_map/dot_general | solution.py:31
  265.0 10.8 %shard_map.324 = bf16[2,2,72,768]{3,2,1,0:T(8,128)(2,1)} custom-call(bf16[1024,2304]{1,0:T(8,128)(2,1)} %fusion.8.k_ref.v_ref.q_ref, bf16[1024,768]{1,0:T(8,128)(2,1)} %convolution_convert_fusion.2.d_ref, f32[1024,768]{1,0:T(8,128)} %get-tuple-element.25.out_ref, f32[1024,768]{1,0:T(8,128)} %get-tuple-element.26.den_ref, ...), custom_call_target="tpu_custom_call" | custom-call | flops 402653184 | bytes 8388608 | tf_op jit(solution)/shard_map/pallas_call | solution.py:255
  277.1 2.4 constant_dynamic-update-slice_fusion.7
  279.4 4.2 fusion.63
  285.4 2.6 constant_dynamic-update-slice_fusion.5
  292.7 4.8 constant_dynamic-update-slice_fusion.2
  297.6 5.1 %dynamic-slice_bitcast_fusion = bf16[2,2,4,216,768]{4,3,2,1,0:T(8,128)(2,1)} fusion(bf16[2,2,2,4,216,768]{5,4,3,2,1,0:T(8,128)(2,1)} %constant_dynamic-update-slice_fusion.2, s32[]{:T(128)S(6)} %select_n.119), kind=kLoop, calls=%fused_computation.13 | loop fusion | bytes 10616836 | tf_op jit(solution)/shard_map/jit(dynamic_index_in_dim)/squeeze | solution.py:316
  303.0 13.1 %collective-permute-done.3 = bf16[2,2,72,768]{3,2,1,0:T(8,128)(2,1)S(1)} collective-permute-done((bf16[2,2,72,768]{3,2,1,0:T(8,128)(2,1)S(1)}, bf16[2,2,72,768]{3,2,1,0:T(8,128)(2,1)S(1)}, u32[]{:S(2)}, u32[]{:S(2)}) %collective-permute-start.3) | collective-permute-done | bytes 442400 | tf_op jit(solution)/shard_map/ppermute | solution.py:287
  318.1 30.5 %shard_map.325 = (bf16[1024,768]{1,0:T(8,128)(2,1)}, bf16[1024,768]{1,0:T(8,128)(2,1)}, bf16[1024,768]{1,0:T(8,128)(2,1)}) custom-call(bf16[1024,2304]{1,0:T(8,128)(2,1)} %fusion.8.k_ref.v_ref.q_ref, bf16[1024,2304]{1,0:T(8,128)(2,1)} %fusion.8.k_ref.v_ref.q_ref, bf16[1024,2304]{1,0:T(8,128)(2,1)} %fusion.8.k_ref.v_ref.q_ref, ...), custom_call_target="tpu_custom_call" | custom-call | flops 12079595520 | bytes 8388608 | tf_op jit(solution)/shard_map/pallas_call | solution.py:265
  348.5 4.5 convolution_convert_fusion.4
  353.0 2.6 convolution_convert_fusion.5
  355.6 2.5 convolution_convert_fusion.6
  363.8 2.3 pad_maximum_fusion.1
  369.1 3.3 fusion.73
  378.5 3.1 add_add_fusion
  381.6 9.7 %collective-permute-done.5 = bf16[2,4,40,768]{3,2,1,0:T(8,128)(2,1)S(1)} collective-permute-done((bf16[2,4,40,768]{3,2,1,0:T(8,128)(2,1)S(1)}, bf16[2,4,40,768]{3,2,1,0:T(8,128)(2,1)S(1)}, u32[]{:S(2)}, u32[]{:S(2)}) %collective-permute-start.5) | collective-permute-done | bytes 491552 | tf_op jit(solution)/shard_map/ppermute | solution.py:305
  393.8 5.0 %collective-permute-done.6 = bf16[4,40,768]{2,1,0:T(8,128)(2,1)S(1)} collective-permute-done((bf16[4,40,768]{2,1,0:T(8,128)(2,1)S(1)}, bf16[4,40,768]{2,1,0:T(8,128)(2,1)S(1)}, u32[]{:S(2)}, u32[]{:S(2)}) %collective-permute-start.6) | collective-permute-done | bytes 245792 | tf_op jit(solution)/shard_map/ppermute | solution.py:305
  398.8 5.4 %fusion.7 = bf16[2,2,4,216,768]{4,3,2,1,0:T(8,128)(2,1)S(1)} fusion(bf16[2,2,4,216,768]{4,3,2,1,0:T(8,128)(2,1)} %collective-permute-done.15, bf16[2,2,2,4,216,768]{5,4,3,2,1,0:T(8,128)(2,1)} %constant_dynamic-update-slice_fusion.2, s32[]{:T(128)S(6)} %select_n.118), kind=kLoop, calls=%fused_computation.11 | loop fusion | flops 10616832 | bytes 15925252 | tf_op jit(solution)/shard_map/convert_element_type | solution.py:317
  416.7 3.1 collective-permute-done.12
  419.8 13.3 %collective-permute-done.21 = bf16[2,4,104,768]{3,2,1,0:T(8,128)(2,1)S(1)} collective-permute-done((bf16[2,4,104,768]{3,2,1,0:T(8,128)(2,1)S(1)}, bf16[2,4,104,768]{3,2,1,0:T(8,128)(2,1)S(1)}, u32[]{:S(2)}, u32[]{:S(2)}) %collective-permute-start.21) | collective-permute-done | bytes 1277984 | tf_op jit(solution)/shard_map/ppermute | solution.py:305
  434.0 6.6 %collective-permute-done.16 = bf16[2,4,112,768]{3,2,1,0:T(8,128)(2,1)S(1)} collective-permute-done((bf16[2,4,112,768]{3,2,1,0:T(8,128)(2,1)S(1)}, bf16[2,4,112,768]{3,2,1,0:T(8,128)(2,1)S(1)}, u32[]{:S(2)}, u32[]{:S(2)}) %collective-permute-start.16) | collective-permute-done | bytes 1376288 | tf_op jit(solution)/shard_map/ppermute | solution.py:305
  443.8 7.2 %collective-permute-done.22 = bf16[4,104,768]{2,1,0:T(8,128)(2,1)S(1)} collective-permute-done((bf16[4,104,768]{2,1,0:T(8,128)(2,1)S(1)}, bf16[4,104,768]{2,1,0:T(8,128)(2,1)S(1)}, u32[]{:S(2)}, u32[]{:S(2)}) %collective-permute-start.22) | collective-permute-done | bytes 639008 | tf_op jit(solution)/shard_map/ppermute | solution.py:305
  451.2 2.4 collective-permute-start.25
  456.2 2.2 collective-permute-start.20
  462.6 12.8 %collective-permute-done.24 = bf16[104,768]{1,0:T(8,128)(2,1)S(1)} collective-permute-done((bf16[104,768]{1,0:T(8,128)(2,1)S(1)}, bf16[104,768]{1,0:T(8,128)(2,1)S(1)}, u32[]{:S(2)}, u32[]{:S(2)}) %collective-permute-start.24) | collective-permute-done | bytes 159776 | tf_op jit(solution)/shard_map/ppermute | solution.py:337
  476.2 4.2 collective-permute-done.19
  (213 shorter events, 74.8 us)
Async XLA Ops:
  7.2 72.1 %all-gather.5.cloned.1.call-start = ((), (), s32[]{:S(2)}) async-start(), calls=%async_computation | async-start | bytes 4055040 | tf_op jit(solution)/shard_map/all_gather | solution.py:399
  15.5 164.6 %all-gather.7.cloned.1.call-start = ((), (), s32[]{:S(2)}) async-start(), calls=%async_computation.1 | async-start | bytes 10948608 | tf_op jit(solution)/shard_map/all_gather | solution.py:400
  83.0 6.2 %copy-start.5 = (bf16[32,24,768]{2,1,0:T(8,128)(2,1)}, bf16[32,24,768]{2,1,0:T(8,128)(2,1)S(1)}, u32[]{:S(2)}) copy-start(bf16[32,24,768]{2,1,0:T(8,128)(2,1)S(1)} %get-tuple-element.106) | copy-start | bytes 3538948
  83.1 6.2 %copy-start.19 = (bf16[32,24,768]{2,1,0:T(8,128)(2,1)}, bf16[32,24,768]{2,1,0:T(8,128)(2,1)S(1)}, u32[]{:S(2)}) copy-start(bf16[32,24,768]{2,1,0:T(8,128)(2,1)S(1)} %get-tuple-element.105) | copy-start | bytes 3538948
  83.1 6.2 %copy-start.21 = (bf16[32,24,768]{2,1,0:T(8,128)(2,1)}, bf16[32,24,768]{2,1,0:T(8,128)(2,1)S(1)}, u32[]{:S(2)}) copy-start(bf16[32,24,768]{2,1,0:T(8,128)(2,1)S(1)} %get-tuple-element.107) | copy-start | bytes 3538948
  100.5 19.3 %collective-permute-start = (bf16[2,2,72,768]{3,2,1,0:T(8,128)(2,1)}, bf16[2,2,72,768]{3,2,1,0:T(8,128)(2,1)S(1)}, u32[]{:S(2)}, u32[]{:S(2)}) collective-permute-start(bf16[2,2,72,768]{3,2,1,0:T(8,128)(2,1)} %shard_map.322), channel_id=1, source_target_pairs={{0,1},{1,2},{2,3},{4,5},{5,6},{6,7},{8,9},{9,10},{10,11},{12,13},{... | collective-permute-start | bytes 1327112 | tf_op jit(solution)/shard_map/ppermute | solution.py:287
  120.9 16.4 %collective-permute-start.1 = (bf16[2,2,72,768]{3,2,1,0:T(8,128)(2,1)S(1)}, bf16[2,2,72,768]{3,2,1,0:T(8,128)(2,1)S(1)}, u32[]{:S(2)}, u32[]{:S(2)}) collective-permute-start(bf16[2,2,72,768]{3,2,1,0:T(8,128)(2,1)S(1)} %fusion.33), channel_id=1, source_target_pairs={{0,2},{1,3},{4,6},{5,7},{8,10},{9,11},{12,14},{13,15},{16,18},{17,... | collective-permute-start | bytes 1327112 | tf_op jit(solution)/shard_map/ppermute | solution.py:287
  129.2 2.6 copy-start
  182.8 3.3 copy-start.25
  182.8 3.6 copy-start.27
  213.4 16.0 %copy-start.14 = (bf16[32,24,768]{2,1,0:T(8,128)(2,1)S(1)}, bf16[32,24,768]{2,1,0:T(8,128)(2,1)}, u32[]{:S(2)}) copy-start(bf16[32,24,768]{2,1,0:T(8,128)(2,1)} %copy-done.13) | copy-start | bytes 3538948
  213.5 16.0 %copy-start.16 = (bf16[32,24,768]{2,1,0:T(8,128)(2,1)S(1)}, bf16[32,24,768]{2,1,0:T(8,128)(2,1)}, u32[]{:S(2)}) copy-start(bf16[32,24,768]{2,1,0:T(8,128)(2,1)} %copy-done.15) | copy-start | bytes 3538948
  213.5 16.0 %copy-start.18 = (bf16[32,24,768]{2,1,0:T(8,128)(2,1)S(1)}, bf16[32,24,768]{2,1,0:T(8,128)(2,1)}, u32[]{:S(2)}) copy-start(bf16[32,24,768]{2,1,0:T(8,128)(2,1)} %copy-done.17) | copy-start | bytes 3538948
  239.6 2.6 copy-start.28
  239.6 5.1 %slice-start = ((s8[6291456]{0:T(1024)(128)(4,1)}), s8[4194304]{0:T(1024)(128)(4,1)S(1)}, s32[]{:S(2)}) async-start(s8[6291456]{0:T(1024)(128)(4,1)} %bitcast.246), calls=%async_computation.2 | async-start | bytes 8388608
  275.8 14.5 %collective-permute-start.2 = (bf16[2,2,72,768]{3,2,1,0:T(8,128)(2,1)}, bf16[2,2,72,768]{3,2,1,0:T(8,128)(2,1)}, u32[]{:S(2)}, u32[]{:S(2)}) collective-permute-start(bf16[2,2,72,768]{3,2,1,0:T(8,128)(2,1)} %shard_map.324), channel_id=1, source_target_pairs={{1,0},{2,1},{3,2},{5,4},{6,5},{7,6},{9,8},{10,9},{11,10},{13,12},{... | collective-permute-start | bytes 1327112 | tf_op jit(solution)/shard_map/ppermute | solution.py:287
  285.4 2.6 copy-start.4
  285.4 3.7 copy-start.3
  285.4 4.9 %copy-start.7 = (bf16[2,2,72,768]{3,2,1,0:T(8,128)(2,1)S(1)}, bf16[2,2,72,768]{3,2,1,0:T(8,128)(2,1)}, u32[]{:S(2)}) copy-start(bf16[2,2,72,768]{3,2,1,0:T(8,128)(2,1)} %shard_map.324) | copy-start | bytes 1327108
  291.4 24.6 %collective-permute-start.3 = (bf16[2,2,72,768]{3,2,1,0:T(8,128)(2,1)S(1)}, bf16[2,2,72,768]{3,2,1,0:T(8,128)(2,1)S(1)}, u32[]{:S(2)}, u32[]{:S(2)}) collective-permute-start(bf16[2,2,72,768]{3,2,1,0:T(8,128)(2,1)S(1)} %fusion.34), channel_id=1, source_target_pairs={{2,0},{3,1},{6,4},{7,5},{10,8},{11,9},{14,12},{15,13},{18,16},{19,... | collective-permute-start | bytes 1327112 | tf_op jit(solution)/shard_map/ppermute | solution.py:287
  302.7 96.1 %collective-permute-start.15 = (bf16[2,2,4,216,768]{4,3,2,1,0:T(8,128)(2,1)}, bf16[2,2,4,216,768]{4,3,2,1,0:T(8,128)(2,1)}, u32[]{:S(2)}, u32[]{:S(2)}) collective-permute-start(bf16[2,2,4,216,768]{4,3,2,1,0:T(8,128)(2,1)} %dynamic-slice_bitcast_fusion), channel_id=1, source_target_pairs={{0,4},{4,0},{8,12},{12,8},{16,20},{20,16},{24,28},{28,24},{1,5},{5... | collective-permute-start | bytes 15925256 | tf_op jit(solution)/shard_map/ppermute | solution.py:305
  348.5 4.5 copy-start.10
  348.5 4.5 copy-start.26
  353.0 2.6 copy-start.8
  358.1 5.4 %copy-start.23 = (bf16[32,24]{1,0:T(8,128)(2,1)S(1)}, bf16[32,24]{1,0:T(8,128)(2,1)}, u32[]{:S(2)}) copy-start(bf16[32,24]{1,0:T(8,128)(2,1)} %reshape.579) | copy-start | bytes 4612
  369.1 4.8 collective-permute-start.4
  369.1 3.3 copy-start.9
  369.1 3.3 copy-start.20
  376.3 15.8 %collective-permute-start.10 = (bf16[2,4,40,768]{3,2,1,0:T(8,128)(2,1)S(1)}, bf16[2,4,40,768]{3,2,1,0:T(8,128)(2,1)S(1)}, u32[]{:S(2)}, u32[]{:S(2)}) collective-permute-start(bf16[2,4,40,768]{3,2,1,0:T(8,128)(2,1)S(1)} %dynamic-slice_bitcast_fusion.5), channel_id=1, source_target_pairs={{0,16},{4,20},{8,24},{12,28},{16,0},{20,4},{24,8},{28,12},{1,17},{... | collective-permute-start | bytes 1474568 | tf_op jit(solution)/shard_map/ppermute | solution.py:305
  377.9 13.4 %collective-permute-start.5 = (bf16[2,4,40,768]{3,2,1,0:T(8,128)(2,1)S(1)}, bf16[2,4,40,768]{3,2,1,0:T(8,128)(2,1)S(1)}, u32[]{:S(2)}, u32[]{:S(2)}) collective-permute-start(bf16[2,4,40,768]{3,2,1,0:T(8,128)(2,1)S(1)} %dynamic-slice_bitcast_fusion.6), channel_id=1, source_target_pairs={{0,8},{4,12},{8,0},{12,4},{16,24},{20,28},{24,16},{28,20},{1,9},{5... | collective-permute-start | bytes 1474568 | tf_op jit(solution)/shard_map/ppermute | solution.py:305
  391.5 7.3 %collective-permute-start.6 = (bf16[4,40,768]{2,1,0:T(8,128)(2,1)S(1)}, bf16[4,40,768]{2,1,0:T(8,128)(2,1)S(1)}, u32[]{:S(2)}, u32[]{:S(2)}) collective-permute-start(bf16[4,40,768]{2,1,0:T(8,128)(2,1)S(1)} %dynamic-slice_bitcast_fusion.8), channel_id=1, source_target_pairs={{0,16},{4,20},{8,24},{12,28},{16,0},{20,4},{24,8},{28,12},{1,17},{... | collective-permute-start | bytes 737288 | tf_op jit(solution)/shard_map/ppermute | solution.py:305
  392.3 15.2 %collective-permute-start.11 = (bf16[4,40,768]{2,1,0:T(8,128)(2,1)S(1)}, bf16[4,40,768]{2,1,0:T(8,128)(2,1)S(1)}, u32[]{:S(2)}, u32[]{:S(2)}) collective-permute-start(bf16[4,40,768]{2,1,0:T(8,128)(2,1)S(1)} %dynamic-slice_bitcast_fusion.7), channel_id=1, source_target_pairs={{0,8},{4,12},{8,0},{12,4},{16,24},{20,28},{24,16},{28,20},{1,9},{5... | collective-permute-start | bytes 737288 | tf_op jit(solution)/shard_map/ppermute | solution.py:305
  404.5 28.6 %collective-permute-start.21 = (bf16[2,4,104,768]{3,2,1,0:T(8,128)(2,1)S(1)}, bf16[2,4,104,768]{3,2,1,0:T(8,128)(2,1)S(1)}, u32[]{:S(2)}, u32[]{:S(2)}) collective-permute-start(bf16[2,4,104,768]{3,2,1,0:T(8,128)(2,1)S(1)} %dynamic-slice_bitcast_fusion.2), channel_id=1, source_target_pairs={{0,16},{4,20},{8,24},{12,28},{16,0},{20,4},{24,8},{28,12},{1,17},{... | collective-permute-start | bytes 3833864 | tf_op jit(solution)/shard_map/ppermute | solution.py:305
  405.1 5.9 %collective-permute-start.9 = (bf16[40,768]{1,0:T(8,128)(2,1)S(1)}, bf16[40,768]{1,0:T(8,128)(2,1)S(1)}, u32[]{:S(2)}, u32[]{:S(2)}) collective-permute-start(bf16[40,768]{1,0:T(8,128)(2,1)S(1)} %get-tuple-element.125), channel_id=1, source_target_pairs={{0,3},{1,0},{2,1},{3,2},{4,7},{5,4},{6,5},{7,6},{8,11},{9,8},{10,9... | collective-permute-start | bytes 184328 | tf_op jit(solution)/shard_map/ppermute | solution.py:337
  405.2 6.3 %collective-permute-start.8 = (bf16[40,768]{1,0:T(8,128)(2,1)S(1)}, bf16[40,768]{1,0:T(8,128)(2,1)S(1)}, u32[]{:S(2)}, u32[]{:S(2)}) collective-permute-start(bf16[40,768]{1,0:T(8,128)(2,1)S(1)} %get-tuple-element.126), channel_id=1, source_target_pairs={{0,2},{1,3},{2,0},{3,1},{4,6},{5,7},{6,4},{7,5},{8,10},{9,11},{10,... | collective-permute-start | bytes 184328 | tf_op jit(solution)/shard_map/ppermute | solution.py:337
  405.3 8.4 %collective-permute-start.7 = (bf16[40,768]{1,0:T(8,128)(2,1)S(1)}, bf16[40,768]{1,0:T(8,128)(2,1)S(1)}, u32[]{:S(2)}, u32[]{:S(2)}) collective-permute-start(bf16[40,768]{1,0:T(8,128)(2,1)S(1)} %get-tuple-element.124), channel_id=1, source_target_pairs={{0,1},{1,2},{2,3},{3,0},{4,5},{5,6},{6,7},{7,4},{8,9},{9,10},{10,1... | collective-permute-start | bytes 184328 | tf_op jit(solution)/shard_map/ppermute | solution.py:337
  407.5 33.1 %collective-permute-start.16 = (bf16[2,4,112,768]{3,2,1,0:T(8,128)(2,1)S(1)}, bf16[2,4,112,768]{3,2,1,0:T(8,128)(2,1)S(1)}, u32[]{:S(2)}, u32[]{:S(2)}) collective-permute-start(bf16[2,4,112,768]{3,2,1,0:T(8,128)(2,1)S(1)} %dynamic-slice_bitcast_fusion.1), channel_id=1, source_target_pairs={{0,8},{4,12},{8,0},{12,4},{16,24},{20,28},{24,16},{28,20},{1,9},{5... | collective-permute-start | bytes 4128776 | tf_op jit(solution)/shard_map/ppermute | solution.py:305
  411.0 4.6 collective-permute-start.14
  411.5 5.1 %collective-permute-start.13 = (bf16[40,768]{1,0:T(8,128)(2,1)S(1)}, bf16[40,768]{1,0:T(8,128)(2,1)S(1)}, u32[]{:S(2)}, u32[]{:S(2)}) collective-permute-start(bf16[40,768]{1,0:T(8,128)(2,1)S(1)} %get-tuple-element.123), channel_id=1, source_target_pairs={{0,2},{1,3},{2,0},{3,1},{4,6},{5,7},{6,4},{7,5},{8,10},{9,11},{10,... | collective-permute-start | bytes 184328 | tf_op jit(solution)/shard_map/ppermute | solution.py:337
  413.7 6.0 %collective-permute-start.12 = (bf16[40,768]{1,0:T(8,128)(2,1)S(1)}, bf16[40,768]{1,0:T(8,128)(2,1)S(1)}, u32[]{:S(2)}, u32[]{:S(2)}) collective-permute-start(bf16[40,768]{1,0:T(8,128)(2,1)S(1)} %get-tuple-element.121), channel_id=1, source_target_pairs={{0,1},{1,2},{2,3},{3,0},{4,5},{5,6},{6,7},{7,4},{8,9},{9,10},{10,1... | collective-permute-start | bytes 184328 | tf_op jit(solution)/shard_map/ppermute | solution.py:337
  433.4 17.6 %collective-permute-start.22 = (bf16[4,104,768]{2,1,0:T(8,128)(2,1)S(1)}, bf16[4,104,768]{2,1,0:T(8,128)(2,1)S(1)}, u32[]{:S(2)}, u32[]{:S(2)}) collective-permute-start(bf16[4,104,768]{2,1,0:T(8,128)(2,1)S(1)} %dynamic-slice_bitcast_fusion.4), channel_id=1, source_target_pairs={{0,8},{4,12},{8,0},{12,4},{16,24},{20,28},{24,16},{28,20},{1,9},{5... | collective-permute-start | bytes 1916936 | tf_op jit(solution)/shard_map/ppermute | solution.py:305
  441.0 14.9 %collective-permute-start.17 = (bf16[4,112,768]{2,1,0:T(8,128)(2,1)S(1)}, bf16[4,112,768]{2,1,0:T(8,128)(2,1)S(1)}, u32[]{:S(2)}, u32[]{:S(2)}) collective-permute-start(bf16[4,112,768]{2,1,0:T(8,128)(2,1)S(1)} %dynamic-slice_bitcast_fusion.3), channel_id=1, source_target_pairs={{0,16},{4,20},{8,24},{12,28},{16,0},{20,4},{24,8},{28,12},{1,17},{... | collective-permute-start | bytes 2064392 | tf_op jit(solution)/shard_map/ppermute | solution.py:305
  451.2 9.6 %collective-permute-start.25 = (bf16[104,768]{1,0:T(8,128)(2,1)S(1)}, bf16[104,768]{1,0:T(8,128)(2,1)S(1)}, u32[]{:S(2)}, u32[]{:S(2)}) collective-permute-start(bf16[104,768]{1,0:T(8,128)(2,1)S(1)} %get-tuple-element.115), channel_id=1, source_target_pairs={{0,3},{1,0},{2,1},{3,2},{4,7},{5,4},{6,5},{7,6},{8,11},{9,8},{10,9... | collective-permute-start | bytes 479240 | tf_op jit(solution)/shard_map/ppermute | solution.py:337
  453.7 21.8 %collective-permute-start.24 = (bf16[104,768]{1,0:T(8,128)(2,1)S(1)}, bf16[104,768]{1,0:T(8,128)(2,1)S(1)}, u32[]{:S(2)}, u32[]{:S(2)}) collective-permute-start(bf16[104,768]{1,0:T(8,128)(2,1)S(1)} %get-tuple-element.116), channel_id=1, source_target_pairs={{0,2},{1,3},{2,0},{3,1},{4,6},{5,7},{6,4},{7,5},{8,10},{9,11},{10,... | collective-permute-start | bytes 479240 | tf_op jit(solution)/shard_map/ppermute | solution.py:337
  454.3 21.1 %collective-permute-start.23 = (bf16[104,768]{1,0:T(8,128)(2,1)S(1)}, bf16[104,768]{1,0:T(8,128)(2,1)S(1)}, u32[]{:S(2)}, u32[]{:S(2)}) collective-permute-start(bf16[104,768]{1,0:T(8,128)(2,1)S(1)} %get-tuple-element.114), channel_id=1, source_target_pairs={{0,1},{1,2},{2,3},{3,0},{4,5},{5,6},{6,7},{7,4},{8,9},{9,10},{10,1... | collective-permute-start | bytes 479240 | tf_op jit(solution)/shard_map/ppermute | solution.py:337
  456.2 20.1 %collective-permute-start.20 = (bf16[112,768]{1,0:T(8,128)(2,1)S(1)}, bf16[112,768]{1,0:T(8,128)(2,1)S(1)}, u32[]{:S(2)}, u32[]{:S(2)}) collective-permute-start(bf16[112,768]{1,0:T(8,128)(2,1)S(1)} %get-tuple-element.112), channel_id=1, source_target_pairs={{0,3},{1,0},{2,1},{3,2},{4,7},{5,4},{6,5},{7,6},{8,11},{9,8},{10,9... | collective-permute-start | bytes 516104 | tf_op jit(solution)/shard_map/ppermute | solution.py:337
  458.4 22.1 %collective-permute-start.19 = (bf16[112,768]{1,0:T(8,128)(2,1)S(1)}, bf16[112,768]{1,0:T(8,128)(2,1)S(1)}, u32[]{:S(2)}, u32[]{:S(2)}) collective-permute-start(bf16[112,768]{1,0:T(8,128)(2,1)S(1)} %get-tuple-element.113), channel_id=1, source_target_pairs={{0,2},{1,3},{2,0},{3,1},{4,6},{5,7},{6,4},{7,5},{8,10},{9,11},{10,... | collective-permute-start | bytes 516104 | tf_op jit(solution)/shard_map/ppermute | solution.py:337
  460.9 19.6 %collective-permute-start.18 = (bf16[112,768]{1,0:T(8,128)(2,1)S(1)}, bf16[112,768]{1,0:T(8,128)(2,1)S(1)}, u32[]{:S(2)}, u32[]{:S(2)}) collective-permute-start(bf16[112,768]{1,0:T(8,128)(2,1)S(1)} %get-tuple-element.111), channel_id=1, source_target_pairs={{0,1},{1,2},{2,3},{3,0},{4,5},{5,6},{6,7},{7,4},{8,9},{9,10},{10,1... | collective-permute-start | bytes 516104 | tf_op jit(solution)/shard_map/ppermute | solution.py:337
  (11 other events, 22.8 us)
Sparse Core Ops, SparseCore 0:
  15.6 63.6 all-gather.4
  82.1 97.9 all-gather.6
